TPU v7x, 256 devices: a whole 4x4x8 slice. The times are simulated.
256 devices in a mesh: row: 8 (over y, core), col: 32 (over x, z).
Axes of the slice: x: 4, y: 4, z: 8, core: 2. Of those that a mesh axis runs over, the one named last changes fastest.
Arguments:
- tokens: bfloat16 [16384, 3072], P(('row', 'col')), may hold values from -6 to 6
- w_in: bfloat16 [3072, 12288], P('row', 'col'), may hold values from -0.109375 to 0.109375
- b_in: float32 [12288], P('col'), may hold values from -3 to 3
- conv_taps: float32 [27, 12288], P(None, 'col'), may hold values from -1.25 to 1.25
- conv_bias: float32 [12288], P('col'), may hold values from -3 to 3
- w_out: bfloat16 [12288, 3072], P('col', 'row'), may hold values from -0.0546875 to 0.0546875
- b_out: float32 [3072], replicated, may hold values from -3 to 3
Outputs:
- mixed: bfloat16 [16384, 3072], P(('row', 'col'))
All inputs are finite; a program needn't handle non-finite values.
Results may differ from a plain program's by a relative error of at most 0.0053.
Values may be sent and summed in bfloat16 or wider, within the bound.
A program may use at most 128 MiB of HBM per device.

v0:
```python
import jax
import jax.numpy as jnp
from jax import lax
from jax.sharding import PartitionSpec as P

HH = 32
WW = 32


def with_halo(shard, sides, width):
    for axis, dim in sides:
        count, length = (lax.axis_size(axis), shard.shape[dim])
        up = [(i, (i + 1) % count) for i in range(count - 1)]
        down = [(j, i) for i, j in up]
        last = lax.slice_in_dim(shard, length - width, length, axis=dim)
        initial = lax.slice_in_dim(shard, 0, width, axis=dim)
        before = lax.ppermute(last, axis, up)
        after = lax.ppermute(initial, axis, down)
        shard = jnp.concatenate([before, shard, after], axis=dim)
    return shard


def body(tokens, w_in, b_in, conv_taps, conv_bias, w_out, b_out):
    own_rows = tokens.shape[0]
    tok_rows = own_rows * lax.axis_size("col")
    hid_cols = w_in.shape[1]
    frame_count = tok_rows // (HH * WW)
    whole = lax.all_gather(tokens, "col", axis=0, tiled=True)
    before = jnp.dot(
        whole, lax.all_gather(w_in, "row", axis=0, tiled=True), preferred_element_type=jnp.float32
    )
    hidden = (before + b_in).astype(jnp.bfloat16).reshape(frame_count, HH, WW, hid_cols)
    extended = with_halo(hidden, (("row", 0),), 1)
    padded = jnp.pad(extended, ((0, 0), (1, 1), (1, 1), (0, 0)))
    summed = jnp.zeros((frame_count, HH, WW, hid_cols), jnp.float32)
    for offset in range(27):
        shift_t = offset // 9
        shift_h = offset // 3 % 3
        shift_w = offset % 3
        window = padded[
            shift_t : shift_t + frame_count, shift_h : shift_h + HH, shift_w : shift_w + WW, :
        ]
        summed = summed + window.astype(jnp.float32) * conv_taps[offset]
    activated = jax.nn.gelu(summed + conv_bias, approximate=True).astype(jnp.bfloat16)
    activated = activated.reshape(tok_rows, hid_cols)
    partial_value = jnp.dot(
        activated,
        lax.all_gather(w_out, "row", axis=1, tiled=True),
        preferred_element_type=jnp.float32,
    )
    shares = lax.psum_scatter(partial_value, "col", scatter_dimension=0, tiled=True)
    return (shares + b_out).astype(jnp.bfloat16)


def solution(mesh):
    placed = (
        P(("row", "col"), None),
        P("row", "col"),
        P("col"),
        P(None, "col"),
        P("col"),
        P("col", "row"),
        P(),
    )
    return jax.shard_map(
        body, mesh=mesh, in_specs=placed, out_specs=P(("row", "col"), None), check_vma=False
    )
```

profile of v0, /device:TPU:3, one launch (start us, length us, event | category | flops | bytes accessed | tf_op | source)
XLA Modules:
  0.0 489.4 jit_solution(7462746669944708098)
XLA Ops:
  6.5 0.7 all-gather.6.cloned.1.call-update
  7.3 0.0 all-gather.4.cloned.1.call-start
  7.3 0.7 all-gather.4.cloned.1.call-update
  8.0 0.0 all-gather.8.cloned.1.call-start
  8.1 32.6 %all-gather.6.cloned.1.call-done = bf16[3072,384]{1,0:T(8,128)(2,1)} async-done(((bf16[384,384]{1,0:T(8,128)(2,1)}), bf16[3072,384]{1,0:T(8,128)(2,1)}) %all-gather.6.cloned.1.call-update) | async-done | bytes 2359312 | tf_op jit(solution)/shard_map/all_gather | solution.py:30
  40.7 119.5 %all-gather.4.cloned.1.call-done = bf16[2048,3072]{1,0:T(8,128)(2,1)} async-done(((bf16[64,3072]{1,0:T(8,128)(2,1)}), bf16[2048,3072]{1,0:T(8,128)(2,1)}) %all-gather.4.cloned.1.call-update) | async-done | bytes 12582928 | tf_op jit(solution)/shard_map/all_gather | solution.py:28
  160.2 10.4 %add_convert_fusion = bf16[2048,384]{1,0:T(8,128)(2,1)S(1)} fusion(bf16[2048,3072]{1,0:T(8,128)(2,1)} %all-gather.4.cloned.1.call-done, bf16[3072,384]{1,0:T(8,128)(2,1)} %all-gather.6.cloned.1.call-done, f32[384]{0:T(512)} %param.9), kind=kOutput, calls=%fused_computation.21 | convolution fusion | flops 4833411072 | bytes 16516608 | tf_op jit(solution)/shard_map/dot_general | solution.py:29
  170.6 0.0 copy-start.2
  170.6 1.3 fusion.14
  171.9 3.3 collective-permute-start.1
  175.2 3.0 collective-permute-start
  178.3 0.0 all-gather.8.cloned.1.call-update
  178.3 0.0 reduce-scatter.2.cloned.1.call-start
  178.3 0.0 copy-done.2
  178.4 0.1 slice_reduce_fusion.26
  178.5 7.7 %collective-permute-done.1 = bf16[1,32,32,384]{3,2,1,0:T(8,128)(2,1)S(1)} collective-permute-done((bf16[1,32,32,384]{3,2,1,0:T(8,128)(2,1)}, bf16[1,32,32,384]{3,2,1,0:T(8,128)(2,1)S(1)}, u32[]{:S(2)}, u32[]{:S(2)}) %collective-permute-start.1) | collective-permute-done | bytes 786464 | tf_op jit(solution)/shard_map/ppermute | solution.py:18
  186.2 1.3 collective-permute-done
  187.5 1.9 select_maximum_fusion
  189.4 14.5 %fusion.13 = bf16[2,32,32,384]{3,2,1,0:T(8,128)(2,1)S(1)} fusion(bf16[2,32,32,384]{3,2,1,0:T(8,128)(2,1)S(1)} %bitcast.9, bf16[4,34,34,384]{3,2,1,0:T(8,128)(2,1)S(1)} %select_maximum_fusion, bf16[1,32,32,384]{3,2,1,0:T(8,128)(2,1)} %copy-done, bf16[1,32,32,384]{3,2,1,0:T(8,128)(2,1)} %copy-done.1, f32[384]{0:T(512)S(1)} %copy-done.4, ...), kind=kLoop, calls=%fused_computation.20 | loop fusion | flops 72351744 | bytes 42510336 | tf_op jit(solution)/shard_map/convert_element_type | solution.py:44
  203.9 1.1 all-gather.8.cloned.1.call-done
  205.1 13.3 %fusion.15 = f32[2048,3072]{1,0:T(8,128)} fusion(bf16[2048,384]{1,0:T(8,128)(2,1)S(1)} %bitcast.10, bf16[384,3072]{1,0:T(8,128)(2,1)} %all-gather.8.cloned.1.call-done), kind=kOutput, calls=%fused_computation.53 | convolution fusion | flops 4831838208 | bytes 29097984 | tf_op jit(solution)/shard_map/dot_general | solution.py:46
  218.4 0.0 reduce-scatter.2.cloned.1.call-update
  218.4 262.5 %reduce-scatter.2.cloned.1.call-done = f32[64,3072]{1,0:T(8,128)} async-done(((f32[2048,3072]{1,0:T(8,128)}), f32[64,3072]{1,0:T(8,128)}) %reduce-scatter.2.cloned.1.call-update) | async-done | bytes 786448 | tf_op jit(solution)/shard_map/reduce_scatter | solution.py:51
  481.0 1.9 add_convert_fusion.1
  (10 shorter events, 0.1 us)
Async XLA Ops:
  6.5 34.2 %all-gather.6.cloned.1.call-start = ((), (), s32[]{:S(2)}) async-start(), calls=%async_computation.2 | async-start | bytes 2654208 | tf_op jit(solution)/shard_map/all_gather | solution.py:30
  7.3 152.9 %all-gather.4.cloned.1.call-start = ((), (), s32[]{:S(2)}) async-start(), calls=%async_computation.1 | async-start | bytes 12976128 | tf_op jit(solution)/shard_map/all_gather | solution.py:28
  8.0 197.1 %all-gather.8.cloned.1.call-start = ((), (), s32[]{:S(2)}) async-start(), calls=%async_computation.3 | async-start | bytes 2654208 | tf_op jit(solution)/shard_map/all_gather | solution.py:48
  170.6 7.7 %copy-start.2 = (f32[27,384]{1,0:T(8,128)S(1)}, f32[27,384]{1,0:T(8,128)}, u32[]{:S(2)}) copy-start(f32[27,384]{1,0:T(8,128)} %param.10) | copy-start | bytes 124420
  171.9 14.3 %collective-permute-start.1 = (bf16[1,32,32,384]{3,2,1,0:T(8,128)(2,1)}, bf16[1,32,32,384]{3,2,1,0:T(8,128)(2,1)S(1)}, u32[]{:S(2)}, u32[]{:S(2)}) collective-permute-start(bf16[1,32,32,384]{3,2,1,0:T(8,128)(2,1)} %bitcast.2), channel_id=1, source_target_pairs={{32,0},{64,32},{96,64},{128,96},{160,128},{192,160},{224,192},{33,... | collective-permute-start | bytes 2359304 | tf_op jit(solution)/shard_map/ppermute | solution.py:18
  175.2 12.2 %collective-permute-start = (bf16[1,32,32,384]{3,2,1,0:T(8,128)(2,1)}, bf16[1,32,32,384]{3,2,1,0:T(8,128)(2,1)S(1)}, u32[]{:S(2)}, u32[]{:S(2)}) collective-permute-start(bf16[1,32,32,384]{3,2,1,0:T(8,128)(2,1)} %bitcast), channel_id=1, source_target_pairs={{0,32},{32,64},{64,96},{96,128},{128,160},{160,192},{192,224},{1,3... | collective-permute-start | bytes 2359304 | tf_op jit(solution)/shard_map/ppermute | solution.py:17
  178.3 302.7 %reduce-scatter.2.cloned.1.call-start = ((), (), s32[]{:S(2)}) async-start(), calls=%async_computation.4 | async-start | bytes 25952256 | tf_op jit(solution)/shard_map/reduce_scatter | solution.py:51
  186.2 3.2 copy-start
  187.5 1.9 copy-start.1
  187.5 1.9 copy-start.4
  218.4 262.6 %copy-start.3 = (f32[3072]{0:T(1024)S(1)}, f32[3072]{0:T(1024)}, u32[]{:S(2)}) copy-start(f32[3072]{0:T(1024)} %param.13) | copy-start | bytes 36868
Sparse Core Ops, SparseCore 0:
  9.2 31.4 all-gather.5
  43.3 116.8 all-gather.3
  178.4 26.6 all-gather.7
  218.5 262.3 reduce-scatter.1
where the time goes:
time: 495 us; the launch traced here: 489 us
  waiting for transfers between devices  426 us (86%)
  matrix products  23.7 us (5%)
  other arithmetic  18.3 us (4%)
  between operations  13.2 us (3%)
  starting transfers between devices  6.43 us (1%)
    reduce_scatter x1, waiting for transfers between devices, body(): lax.psum_scatter(partial_value, 'col', scatter_dimension=0, tiled=True)  263 us
    all_gather x1, waiting for transfers between devices, body(): whole = lax.all_gather(tokens, 'col', axis=0, tiled=True)  119 us
    all_gather x1, waiting for transfers between devices, body(): lax.all_gather(w_in, 'row', axis=0, tiled=True)  32.6 us
    convert_element_type x1, other arithmetic, body(): jax.nn.gelu(summed + conv_bias, approximate=True).astype(jnp.bfloat16)  14.5 us
    dot_general x1, matrix products, body(): jnp.dot(activated, lax.all_gather(w_out, 'row', axis=1, tiled=True), pref...  13.3 us
    dot_general x1, matrix products, body(): jnp.dot(whole, lax.all_gather(w_in, 'row', axis=0, tiled=True), preferred...  10.4 us
  transfers between devices with their start and end apart: 6, of which 6 were waited for; matrix products, arithmetic and copies ran while one was open for 3% of the time, Pallas kernels for 0%

commit v1 on v0

v1 whole, which is shorter than its diff:
```python
import functools

import jax
import jax.numpy as jnp
from jax import lax
from jax.experimental import pallas as pl
from jax.experimental.pallas import tpu as pltpu
from jax.sharding import PartitionSpec as P

MESH = pl.DeviceIdType.MESH
NX, NY, NZ = 4, 4, 8
D = 3072
BLK = 384
HALF = BLK // 2
CH = NX * BLK
GROUP = 512
OWN = 64
WW = 32
ROWS = GROUP // WW
HALO_CHUNKS = 3
HALO_CH = CH // HALO_CHUNKS
BF16, F32 = jnp.bfloat16, jnp.float32


def place():
    row, col = lax.axis_index("row"), lax.axis_index("col")
    return row // 2, row % 2, col // NZ, col % NZ


def dev(y, c, x, z):
    return {"row": y * 2 + c, "col": x * NZ + z}


def moved_to(y, c, x):
    b = c ^ (y & 1)
    upper = x & 1
    return x >> 1, jnp.where(upper == 0, b, 3 - b)


def moved_from(y, c, x):
    b = (x ^ (x >> 1)) & 1
    return b ^ (y & 1), c * 2 + (x >> 1)


def frame_of(y, c, x):
    b = (x ^ (x >> 1)) & 1
    return 4 * y + 2 * (b ^ (y & 1)) + c


def holder(frame, upper):
    pair = frame >> 1
    y = pair >> 1
    b = (pair & 1) ^ (y & 1)
    return y, frame & 1, jnp.where(upper == 0, b, 3 - b)


class Sender:
    def __init__(self, ssem, rsem):
        self.ssem, self.rsem, self.used, self.sent = ssem, rsem, 0, []

    def key(self):
        self.used += 1
        return self.used - 1

    def make(self, src, dst, k, to):
        return pltpu.make_async_remote_copy(
            src_ref=src,
            dst_ref=dst,
            send_sem=self.ssem.at[k],
            recv_sem=self.rsem.at[k],
            device_id=to,
            device_id_type=MESH,
        )

    def send(self, src, dst, to, when=None):
        k = self.key()
        copy = self.make(src, dst, k, to)
        if when is None:
            copy.start()
        else:
            pl.when(when)(copy.start)
        self.sent.append((copy, when))
        return k

    def arrived(self, ref, k, when=None):
        copy = pltpu.make_async_copy(ref, ref, self.rsem.at[k])
        if when is None:
            copy.wait()
        else:
            pl.when(when)(copy.wait)

    def drain(self):
        for copy, when in self.sent:
            if when is None:
                copy.wait_send()
            else:
                pl.when(when)(copy.wait_send)
        self.sent = []


def greet(peers):
    barrier = pltpu.get_barrier_semaphore()
    count = 0
    for to, when in peers:
        signal = functools.partial(pl.semaphore_signal, barrier, inc=1, device_id=to, device_id_type=MESH)
        if when is None:
            signal()
            count = count + 1
        else:
            pl.when(when)(signal)
            count = count + when.astype(jnp.int32)
    pl.semaphore_wait(barrier, count)


class WeightGather:
    def __init__(self, sender, own, block, band_a, band_b):
        self.s, self.own = sender, own
        self.block, self.band_a, self.band_b = block, band_a, band_b
        self.y, self.c, self.x, self.z = place()
        self.xp, self.xm = (self.x + 1) % NX, (self.x + NX - 1) % NX
        self.yp, self.ym = (self.y + 1) % NY, (self.y + NY - 1) % NY
        self.x2, self.y2 = (self.x + 2) % NX, (self.y + 2) % NY

    def to_x(self, x):
        return dev(self.y, self.c, x, self.z)

    def to_y(self, y):
        return dev(y, self.c, self.x, self.z)

    def stage1(self):
        s, x, y, own = self.s, self.x, self.y, self.own
        a, b = pl.ds(0, HALF), pl.ds(HALF, HALF)
        self.k_axp = s.send(own.at[a], self.block(x, y, a), self.to_x(self.xp))
        self.k_axm = s.send(own.at[a], self.block(x, y, a), self.to_x(self.xm))
        self.k_byp = s.send(own.at[b], self.block(x, y, b), self.to_y(self.yp))
        self.k_bym = s.send(own.at[b], self.block(x, y, b), self.to_y(self.ym))

    def stage1_forward(self):
        s, q = self.s, HALF // 2
        lo, hi = pl.ds(0, q), pl.ds(q, q)
        s.arrived(self.block(self.xm, self.y, pl.ds(0, HALF)), self.k_axp)
        src = self.block(self.xm, self.y, lo)
        self.k_afp = s.send(src, src, self.to_x(self.xp))
        s.arrived(self.block(self.xp, self.y, pl.ds(0, HALF)), self.k_axm)
        src = self.block(self.xp, self.y, hi)
        self.k_afm = s.send(src, src, self.to_x(self.xm))
        lo, hi = pl.ds(HALF, q), pl.ds(HALF + q, q)
        s.arrived(self.block(self.x, self.ym, pl.ds(HALF, HALF)), self.k_byp)
        src = self.block(self.x, self.ym, lo)
        self.k_bfp = s.send(src, src, self.to_y(self.yp))
        s.arrived(self.block(self.x, self.yp, pl.ds(HALF, HALF)), self.k_bym)
        src = self.block(self.x, self.yp, hi)
        self.k_bfm = s.send(src, src, self.to_y(self.ym))

    def stage2(self):
        s, q = self.s, HALF // 2
        s.arrived(self.block(self.x2, self.y, pl.ds(0, q)), self.k_afp)
        s.arrived(self.block(self.x2, self.y, pl.ds(q, q)), self.k_afm)
        band = self.band_a(self.y, None)
        self.k_ayp = s.send(band, band, self.to_y(self.yp))
        self.k_aym = s.send(band, band, self.to_y(self.ym))
        s.arrived(self.block(self.x, self.y2, pl.ds(HALF, q)), self.k_bfp)
        s.arrived(self.block(self.x, self.y2, pl.ds(HALF + q, q)), self.k_bfm)
        band = self.band_b(self.x, None)
        self.k_bxp = s.send(band, band, self.to_x(self.xp))
        self.k_bxm = s.send(band, band, self.to_x(self.xm))
        self.partner(0, self.y, self.x)

    def partner(self, at, y, x):
        other = dev(self.y, 1 - self.c, self.x, self.z)
        a, b = self.band_a(y, None), self.band_b(x, None)
        ka = self.s.send(a, a, other)
        kb = self.s.send(b, b, other)
        self.from_partner = getattr(self, "from_partner", [])
        self.from_partner.append((ka, kb, y, x))

    def stage2_forward(self):
        s = self.s
        s.arrived(self.band_a(self.ym, None), self.k_ayp)
        src = self.band_a(self.ym, 0)
        self.k_a2p = s.send(src, src, self.to_y(self.yp))
        s.arrived(self.band_a(self.yp, None), self.k_aym)
        src = self.band_a(self.yp, 1)
        self.k_a2m = s.send(src, src, self.to_y(self.ym))
        s.arrived(self.band_b(self.xm, None), self.k_bxp)
        src = self.band_b(self.xm, 0)
        self.k_b2p = s.send(src, src, self.to_x(self.xp))
        s.arrived(self.band_b(self.xp, None), self.k_bxm)
        src = self.band_b(self.xp, 1)
        self.k_b2m = s.send(src, src, self.to_x(self.xm))
        self.partner(1, self.ym, self.xm)
        self.partner(2, self.yp, self.xp)

    def stage3(self):
        s = self.s
        for part, k in ((0, self.k_a2p), (1, self.k_a2m)):
            s.arrived(self.band_a(self.y2, part), k)
        for part, k in ((0, self.k_b2p), (1, self.k_b2m)):
            s.arrived(self.band_b(self.x2, part), k)
        self.partner(3, self.y2, self.x2)

    def finish(self):
        for ka, kb, y, x in self.from_partner:
            self.s.arrived(self.band_a(y, None), ka)
            self.s.arrived(self.band_b(x, None), kb)


def gather_kernel(
    tok_in, win_in, wout_in, par_in, ext_out, wout, par_out, tok, win, ext, par, lsem, ssem, rsem
):
    y, c, x, z = place()
    s = Sender(ssem, rsem)
    xs = [(x + d) % NX for d in range(NX)]
    zp, zm = (z + 1) % NZ, (z + NZ - 1) % NZ
    yp, ym = (y + 1) % NY, (y + NY - 1) % NY
    upper = x >> 1
    frame = frame_of(y, c, x)
    last = NY * 4 - 1
    tc, tx = moved_to(y, c, x)
    fc, fx = moved_from(y, c, x)
    stays = (tc == c) & (tx == x)
    moves = jnp.logical_not(stays)
    has_next, has_prev = frame < last, frame > 0
    ny, nc, nx = holder(jnp.minimum(frame + 1, last), upper)
    py, pc, px = holder(jnp.maximum(frame - 1, 0), upper)
    nxt, nxt_other = dev(ny, nc, nx, z), dev(ny, nc, 3 - nx, z)
    prv, prv_other = dev(py, pc, px, z), dev(py, pc, 3 - px, z)
    other_half = dev(y, c, 3 - x, z)

    greet(
        [(dev(y, c, xs[d], z), None) for d in (1, 2, 3)]
        + [(dev(yp, c, x, z), None), (dev(ym, c, x, z), None)]
        + [(dev(y, c, x, zp), None), (dev(y, c, x, zm), None)]
        + [(dev(y, 1 - c, x, z), None)]
        + [(dev(y, tc, tx, z), moves), (dev(y, fc, fx, z), moves)]
        + [(nxt, has_next), (nxt_other, has_next), (prv, has_prev), (prv_other, has_prev)]
        + [(other_half, None)]
    )

    home = tok.at[pl.ds(z * OWN, OWN)]
    k_move = s.send(tok_in, home, dev(y, tc, tx, z), when=moves)
    stay = pltpu.make_async_copy(tok_in, home, rsem.at[k_move])
    pl.when(stays)(stay.start)

    def par_at(x_):
        return par.at[:, pl.ds(x_ * BLK, BLK)]

    k_par = [s.send(par_in, par_at(x), dev(y, c, xs[d], z)) for d in (1, 2, 3)]
    own_par = pltpu.make_async_copy(par_in, par_at(x), lsem.at[0])
    own_par.start()

    def win_block(x_, y_, rows):
        return win.at[y_, c, rows, pl.ds(x_ * BLK, BLK)]

    def win_a(y_, part):
        cols = pl.ds(0, CH) if part is None else pl.ds(part * (CH // 2), CH // 2)
        return win.at[y_, c, pl.ds(0, HALF), cols]

    def win_b(x_, part):
        ys = pl.ds(0, NY) if part is None else pl.ds(part * 2, 2)
        return win.at[ys, c, pl.ds(HALF, HALF), pl.ds(x_ * BLK, BLK)]

    def wout_block(x_, y_, rows):
        return wout.at[x_, rows, pl.ds(c * (NY * BLK) + y_ * BLK, BLK)]

    def wout_a(y_, part):
        xs_ = pl.ds(0, NX) if part is None else pl.ds(part * 2, 2)
        return wout.at[xs_, pl.ds(0, HALF), pl.ds(c * (NY * BLK) + y_ * BLK, BLK)]

    def wout_b(x_, part):
        n = NY * BLK
        cols = pl.ds(c * n, n) if part is None else pl.ds(c * n + part * (n // 2), n // 2)
        return wout.at[x_, pl.ds(HALF, HALF), cols]

    g_in = WeightGather(s, win_in, win_block, win_a, win_b)
    g_out = WeightGather(s, wout_in, wout_block, wout_a, wout_b)
    own_in = pltpu.make_async_copy(win_in, win_block(x, y, pl.ds(0, BLK)), lsem.at[1])
    own_out = pltpu.make_async_copy(wout_in, wout_block(x, y, pl.ds(0, BLK)), lsem.at[2])
    own_in.start()
    own_out.start()
    g_in.stage1()

    @pl.when(upper == 0)
    def _():
        ext[:, 0] = jnp.zeros((3, WW, CH), BF16)

    @pl.when(upper == 1)
    def _():
        ext[:, ROWS + 1] = jnp.zeros((3, WW, CH), BF16)

    @pl.when(jnp.logical_not(has_prev))
    def _():
        @pl.loop(0, ROWS + 2)
        def _(r):
            ext[0, r] = jnp.zeros((WW, CH), BF16)

    @pl.when(jnp.logical_not(has_next))
    def _():
        @pl.loop(0, ROWS + 2)
        def _(r):
            ext[2, r] = jnp.zeros((WW, CH), BF16)

    piece = OWN // 2

    def tok_at(z_, p):
        return tok.at[pl.ds(((z_ + NZ) % NZ) * OWN + p * piece, piece)]

    k_tok = {}

    def token_step(d):
        for p in (0, 1):
            for way, to in ((1, zp), (-1, zm)):
                if d == 4 and (p == 0) != (way == 1):
                    continue
                src = tok_at(z - way * (d - 1), p)
                if d > 1:
                    s.arrived(src, k_tok[way, d - 1, p])
                k_tok[way, d, p] = s.send(src, src, dev(y, c, x, to))

    stay.wait()
    token_step(1)
    g_in.stage1_forward()
    own_in.wait()
    g_in.stage2()
    token_step(2)
    token_step(3)
    g_in.stage2_forward()
    g_out.stage1()
    own_out.wait()
    token_step(4)
    g_in.stage3()
    g_out.stage1_forward()
    own_par.wait()
    for d in (1, 2, 3):
        s.arrived(par_at((x + NX - d) % NX), k_par[d - 1])
    s.arrived(tok_at(z - 3, 1), k_tok[1, 3, 1])
    s.arrived(tok_at(z + 3, 0), k_tok[-1, 3, 0])
    s.arrived(tok_at(z - 4, 0), k_tok[1, 4, 0])
    s.arrived(tok_at(z + 4, 1), k_tok[-1, 4, 1])
    g_in.finish()

    src_row = jnp.where(upper == 0, ROWS, 1)
    dst_row = jnp.where(upper == 0, 0, ROWS + 1)
    got_row = jnp.where(upper == 0, ROWS + 1, 0)
    inner = pl.ds(1, ROWS)
    arrivals = []
    step = 256
    for j in range(HALO_CHUNKS):

        @pl.loop(0, HALO_CH // step)
        def _(i):
            cols = pl.ds(pl.multiple_of(j * HALO_CH + i * step, step), step)
            w = win[:, :, :, cols].reshape(D, step)
            before = jnp.dot(tok[...], w, preferred_element_type=F32) + par[0:1, cols]
            ext[1, inner, :, cols] = before.astype(BF16).reshape(ROWS, WW, step)

        cols = pl.ds(j * HALO_CH, HALO_CH)
        frame_src = ext.at[1, inner, :, cols]
        row_src = ext.at[1, src_row, :, cols]
        k1 = s.send(frame_src, ext.at[0, inner, :, cols], nxt, when=has_next)
        k2 = s.send(frame_src, ext.at[2, inner, :, cols], prv, when=has_prev)
        k3 = s.send(row_src, ext.at[1, dst_row, :, cols], other_half)
        k4 = s.send(row_src, ext.at[0, dst_row, :, cols], nxt_other, when=has_next)
        k5 = s.send(row_src, ext.at[2, dst_row, :, cols], prv_other, when=has_prev)
        arrivals += [
            (ext.at[0, inner, :, cols], k1, has_prev),
            (ext.at[2, inner, :, cols], k2, has_next),
            (ext.at[1, got_row, :, cols], k3, None),
            (ext.at[0, got_row, :, cols], k4, has_prev),
            (ext.at[2, got_row, :, cols], k5, has_next),
        ]
        if j == 0:
            g_out.stage2()

    par_done = pltpu.make_async_copy(par, par_out, lsem.at[3])
    par_done.start()
    for ref, k, when in arrivals:
        s.arrived(ref, k, when)
    ext_done = pltpu.make_async_copy(ext, ext_out, lsem.at[4])
    ext_done.start()
    g_out.stage2_forward()
    g_out.stage3()
    g_out.finish()
    par_done.wait()
    ext_done.wait()
    s.drain()


def gather(tokens, w_in, w_out, par):
    vmem = pl.BlockSpec(memory_space=pltpu.VMEM)
    hbm = pl.BlockSpec(memory_space=pl.ANY)
    keys = 100
    return pl.pallas_call(
        gather_kernel,
        out_shape=[
            jax.ShapeDtypeStruct((3, ROWS + 2, WW, CH), BF16),
            jax.ShapeDtypeStruct((NX, BLK, D), BF16),
            jax.ShapeDtypeStruct((32, CH), F32),
        ],
        in_specs=[vmem] * 4,
        out_specs=[hbm] * 3,
        scratch_shapes=[
            pltpu.VMEM((GROUP, D), BF16),
            pltpu.VMEM((NY, 2, BLK, CH), BF16),
            pltpu.VMEM((3, ROWS + 2, WW, CH), BF16),
            pltpu.VMEM((32, CH), F32),
            pltpu.SemaphoreType.DMA((8,)),
            pltpu.SemaphoreType.DMA((keys,)),
            pltpu.SemaphoreType.DMA((keys,)),
        ],
        compiler_params=pltpu.CompilerParams(
            collective_id=0, has_side_effects=True, vmem_limit_bytes=48 * 2**20
        ),
        name="gather",
    )(tokens, w_in, w_out, par)


CONV_CH = 256


def conv_kernel(ext, par, w, out, act):
    @pl.when(pl.program_id(0) == 0)
    def _():
        @pl.loop(0, GROUP, step=64)
        def _(r):
            out[pl.ds(r, 64), :] = jnp.zeros((64, D), F32)

    column = lax.broadcasted_iota(jnp.int32, (WW, 128), 0)
    for lc in range(CONV_CH // 128):
        lanes = pl.ds(lc * 128, 128)

        @pl.loop(0, ROWS)
        def _(r):
            sums = [None, None, None]
            for dt in range(3):
                for dh in range(3):
                    v = ext[dt, r + dh, :, lanes].astype(F32)
                    for dw in range(3):
                        t = v * par[1 + 9 * dt + 3 * dh + dw : 2 + 9 * dt + 3 * dh + dw, lanes]
                        sums[dw] = t if sums[dw] is None else sums[dw] + t
            left = jnp.where(column == 0, 0.0, pltpu.roll(sums[0], 1, 0))
            right = jnp.where(column == WW - 1, 0.0, pltpu.roll(sums[2], WW - 1, 0))
            v = sums[1] + left + right + par[28:29, lanes]
            g = 0.5 * v * (1.0 + jnp.tanh(0.7978845608028654 * (v + 0.044715 * v * v * v)))
            act[pl.ds(pl.multiple_of(r * WW, WW), WW), lanes] = g.astype(BF16)

    @pl.loop(0, D // 512)
    def _(n):
        cols = pl.ds(pl.multiple_of(n * 512, 512), 512)
        out[:, cols] += jnp.dot(act[...], w[:, cols], preferred_element_type=F32)


def conv_mlp(ext, par, w_out):
    return pl.pallas_call(
        conv_kernel,
        grid=(CH // CONV_CH,),
        out_shape=jax.ShapeDtypeStruct((GROUP, D), F32),
        in_specs=[
            pl.BlockSpec((3, ROWS + 2, WW, CONV_CH), lambda i: (0, 0, 0, i)),
            pl.BlockSpec((32, CONV_CH), lambda i: (0, i)),
            pl.BlockSpec((CONV_CH, D), lambda i: (i, 0)),
        ],
        out_specs=pl.BlockSpec((GROUP, D), lambda i: (0, 0)),
        scratch_shapes=[pltpu.VMEM((GROUP, CONV_CH), BF16)],
        compiler_params=pltpu.CompilerParams(vmem_limit_bytes=40 * 2**20),
        name="conv_mlp",
    )(ext, par, w_out)


def scatter_kernel(part, bias, out, sendbuf, recvbuf, done, lsem, ssem, rsem):
    y, c, x, z = place()
    s = Sender(ssem, rsem)
    zp, zm = (z + 1) % NZ, (z + NZ - 1) % NZ
    tc, tx = moved_to(y, c, x)
    fc, fx = moved_from(y, c, x)
    stays = (tc == c) & (tx == x)
    moves = jnp.logical_not(stays)
    greet(
        [(dev(y, c, x, zp), None), (dev(y, c, x, zm), None)]
        + [(dev(y, tc, tx, z), moves), (dev(y, fc, fx, z), moves)]
    )
    wide = D // 2
    chains = [(q, way, 4 if (q == 0) == (way == 1) else 3) for q in (0, 1) for way in (1, -1)]
    slot, n = {}, 0
    for i, (q, way, length) in enumerate(chains):
        for step in range(length):
            slot[i, step] = n
            n += 1
    k_of = {}
    for step in range(4):
        for i, (q, way, length) in enumerate(chains):
            if step >= length:
                continue
            at = (z + way * (length - step) + NZ) % NZ
            rows = pl.ds(pl.multiple_of(at * OWN, OWN), OWN)
            value = part[rows, q * wide : (q + 1) * wide]
            if step > 0:
                got = recvbuf.at[slot[i, step - 1]]
                s.arrived(got, k_of[i, step - 1])
                value = value + got[...].astype(F32)
            mine = slot[i, step]
            sendbuf[mine] = value.astype(BF16)
            to = dev(y, c, x, zp if way == 1 else zm)
            k_of[i, step] = s.send(sendbuf.at[mine], recvbuf.at[mine], to)
    rows = pl.ds(pl.multiple_of(z * OWN, OWN), OWN)
    for q in (0, 1):
        value = part[rows, q * wide : (q + 1) * wide]
        for i in (2 * q, 2 * q + 1):
            mine = slot[i, chains[i][2] - 1]
            s.arrived(recvbuf.at[mine], k_of[i, chains[i][2] - 1])
            value = value + recvbuf[mine].astype(F32)
        for y_ in range(NY):
            to = (y_ * 2 + q) * BLK
            done[:, to : to + BLK] = (
                value[:, y_ * BLK : (y_ + 1) * BLK] + bias[:, to : to + BLK]
            ).astype(BF16)
    k = s.send(done, out, dev(y, fc, fx, z), when=moves)
    stay = pltpu.make_async_copy(done, out, rsem.at[k])
    pl.when(stays)(stay.start)
    stay.wait()
    s.drain()


def scatter(part, bias):
    vmem = pl.BlockSpec(memory_space=pltpu.VMEM)
    return pl.pallas_call(
        scatter_kernel,
        out_shape=jax.ShapeDtypeStruct((OWN, D), BF16),
        in_specs=[vmem] * 2,
        out_specs=pl.BlockSpec(memory_space=pl.ANY),
        scratch_shapes=[
            pltpu.VMEM((14, OWN, D // 2), BF16),
            pltpu.VMEM((14, OWN, D // 2), BF16),
            pltpu.VMEM((OWN, D), BF16),
            pltpu.SemaphoreType.DMA((2,)),
            pltpu.SemaphoreType.DMA((16,)),
            pltpu.SemaphoreType.DMA((16,)),
        ],
        compiler_params=pltpu.CompilerParams(
            collective_id=1, has_side_effects=True, vmem_limit_bytes=32 * 2**20
        ),
        name="scatter",
    )(part, bias)


def body(tokens, w_in, b_in, conv_taps, conv_bias, w_out, b_out):
    par = jnp.concatenate([b_in[None], conv_taps, conv_bias[None], jnp.zeros((3, BLK), F32)])
    ext, wide_out, wide_par = gather(tokens, w_in, w_out, par)
    part = conv_mlp(ext, wide_par, wide_out.reshape(CH, D))
    return scatter(part, b_out[None])


def solution(mesh):
    placed = (
        P(("row", "col"), None),
        P("row", "col"),
        P("col"),
        P(None, "col"),
        P("col"),
        P("col", "row"),
        P(),
    )
    return jax.shard_map(
        body, mesh=mesh, in_specs=placed, out_specs=P(("row", "col"), None), check_vma=False
    )
```

time: 495 us -> 178 us (0.36); the launches traced: 489 us -> 178 us
  waiting for transfers between devices: 426 us -> 0 us
  Pallas kernels: 0 us -> 169 us
  matrix products: 23.7 us -> 0 us
  other arithmetic: 18.3 us -> 0.87 us
  between operations: 13.2 us -> 0.05 us
  starting transfers between devices: 6.43 us -> 0 us
  local copies, waits for them, and re-layouts: 1.48 us -> 7.61 us
    reduce_scatter x1 -> x0, waiting for transfers between devices: 263 us -> none  [body(): lax.psum_scatter(partial_value, 'col', scatter_dimension=0, tiled=True)]
    pallas_call x0 -> x3, Pallas kernels: none -> 169 us  [the longest x1 99.7 us: gather(): pl.pallas_call(gather_kernel, out_shape=[jax.ShapeDtypeStruct((3, ROWS +...]
    all_gather x3 -> x0, waiting for transfers between devices: 153 us -> none  [the longest x1 119 us: body(): whole = lax.all_gather(tokens, 'col', axis=0, tiled=True)]
    dot_general x2 -> x0, matrix products: 23.7 us -> none  [the longest x1 13.3 us: body(): jnp.dot(activated, lax.all_gather(w_out, 'row', axis=1, tiled=True), pref...]
    convert_element_type x2 -> x0, other arithmetic: 16.4 us -> none  [the longest x1 14.5 us: body(): jax.nn.gelu(summed + conv_bias, approximate=True).astype(jnp.bfloat16)]
    ppermute x2 -> x0, waiting for transfers between devices: 8.99 us -> none  [the longest x1 7.7 us: with_halo(): after = lax.ppermute(initial, axis, down)]
    ppermute x2 -> x0, starting transfers between devices: 6.31 us -> none  [the longest x1 3.3 us: with_halo(): after = lax.ppermute(initial, axis, down)]
    unnamed x10 -> x11, local copies, waits for them, and re-layouts: 0.02 us -> 6.17 us
  transfers between devices with their start and end apart: 6 -> 0, of which waited for: 6 -> 0; matrix products, arithmetic and copies ran while one was open for 3% -> 0% of each run, Pallas kernels for 0% -> 0%
where the time goes in v1:
time: 178 us
  Pallas kernels  169 us (95%)
  local copies, waits for them, and re-layouts  7.61 us (4%)
    pallas_call x1, Pallas kernels, gather(): pl.pallas_call(gather_kernel, out_shape=[jax.ShapeDtypeStruct((3, ROWS +...  99.7 us
    pallas_call x1, Pallas kernels, scatter(): pl.pallas_call(scatter_kernel, out_shape=jax.ShapeDtypeStruct((OWN, D), B...  44.8 us
    pallas_call x1, Pallas kernels, conv_mlp(): pl.pallas_call(conv_kernel, grid=(CH // CONV_CH,), out_shape=jax.ShapeDty...  24.8 us
    unnamed x11, local copies, waits for them, and re-layouts  6.17 us

profile of v1, /device:TPU:3, one launch (start us, length us, event | category | flops | bytes accessed | tf_op | source)
XLA Modules:
  0.0 177.8 jit_solution(2841138953780078853)
XLA Ops:
  0.0 0.1 pad.3.clone
  0.1 0.7 broadcast_in_dim.12
  0.8 0.7 broadcast_in_dim.13
  1.4 0.9 maximum_maximum_fusion.par_in
  2.3 0.0 copy-start.1
  2.3 1.0 copy-done.1
  3.3 0.0 copy-start.2
  3.3 1.0 copy-done.2
  4.3 0.0 copy-start.3
  4.3 1.0 copy-done.3
  5.2 99.7 %gather.1 = (bf16[3,18,32,1536]{3,2,1,0:T(8,128)(2,1)}, bf16[4,384,3072]{2,1,0:T(8,128)(2,1)}, f32[32,1536]{1,0:T(8,128)S(1)}) custom-call(bf16[64,3072]{1,0:T(8,128)(2,1)S(1)} %copy-done.1, bf16[384,384]{1,0:T(8,128)(2,1)S(1)} %copy-done.2, bf16[384,384]{1,0:T(8,128)(2,1)S(1)} %copy-done.3, f32[32,384]{1,0:T(8,128)S(1)} %maximum_maximum_fusion.par_in), custom_call_target="tpu_custom_call" | custom-call | tf_op jit(solution)/shard_map/gather/pallas_call | solution.py:393
  104.9 0.0 copy-start
  104.9 2.5 %copy-done = bf16[3,18,32,1536]{3,2,1,0:T(8,128)(2,1)S(1)} copy-done((bf16[3,18,32,1536]{3,2,1,0:T(8,128)(2,1)S(1)}, bf16[3,18,32,1536]{3,2,1,0:T(8,128)(2,1)}, u32[]{:S(2)}) %copy-start) | copy-done | bytes 5308440
  107.4 0.0 copy-start.4
  107.4 24.8 %conv_mlp.1.part = f32[512,3072]{1,0:T(8,128)S(1)} custom-call(bf16[3,18,32,1536]{3,2,1,0:T(8,128)(2,1)S(1)} %copy-done, f32[32,1536]{1,0:T(8,128)S(1)} %get-tuple-element.9.par, bf16[1536,3072]{1,0:T(8,128)(2,1)} %bitcast.3), custom_call_target="tpu_custom_call" | custom-call | tf_op jit(solution)/shard_map/conv_mlp/pallas_call | solution.py:454
  132.2 0.0 copy-done.4
  132.2 44.8 %scatter.1 = bf16[64,3072]{1,0:T(8,128)(2,1)S(1)} custom-call(f32[512,3072]{1,0:T(8,128)S(1)} %conv_mlp.1.part, f32[1,3072]{1,0:T(1,128)S(1)} %bitcast.2), custom_call_target="tpu_custom_call" | custom-call | tf_op jit(solution)/shard_map/scatter/pallas_call | solution.py:526
  177.1 0.7 copy.9
  (1 shorter events, 0.0 us)
Async XLA Ops:
  2.3 1.0 copy-start.1
  3.3 1.0 copy-start.2
  4.3 1.0 copy-start.3
  104.9 2.5 %copy-start = (bf16[3,18,32,1536]{3,2,1,0:T(8,128)(2,1)S(1)}, bf16[3,18,32,1536]{3,2,1,0:T(8,128)(2,1)}, u32[]{:S(2)}) copy-start(bf16[3,18,32,1536]{3,2,1,0:T(8,128)(2,1)} %get-tuple-element.8.ext) | copy-start | bytes 15925252
  107.4 24.8 %copy-start.4 = (f32[3072]{0:T(1024)S(1)}, f32[3072]{0:T(1024)}, u32[]{:S(2)}) copy-start(f32[3072]{0:T(1024)} %param.13) | copy-start | bytes 36868

commit v2 on v1

v2 whole, which is shorter than its diff:
```python
import functools

import jax
import jax.numpy as jnp
from jax import lax
from jax.experimental import pallas as pl
from jax.experimental.pallas import tpu as pltpu
from jax.sharding import PartitionSpec as P

MESH = pl.DeviceIdType.MESH
NX, NY, NZ = 4, 4, 8
D = 3072
BLK = 384
HALF = BLK // 2
CH = NX * BLK
GROUP = 512
OWN = 64
WW = 32
ROWS = GROUP // WW
HALO_CHUNKS = 3
PIECES = 4
PIECE = OWN // PIECES
UNIT = 1024
HALO_CH = CH // HALO_CHUNKS
BF16, F32 = jnp.bfloat16, jnp.float32


def place():
    row, col = lax.axis_index("row"), lax.axis_index("col")
    return row // 2, row % 2, col // NZ, col % NZ


def dev(y, c, x, z):
    return {"row": y * 2 + c, "col": x * NZ + z}


def moved_to(y, c, x):
    b = c ^ (y & 1)
    upper = x & 1
    return x >> 1, jnp.where(upper == 0, b, 3 - b)


def moved_from(y, c, x):
    b = (x ^ (x >> 1)) & 1
    return b ^ (y & 1), c * 2 + (x >> 1)


def frame_of(y, c, x):
    b = (x ^ (x >> 1)) & 1
    return 4 * y + 2 * (b ^ (y & 1)) + c


def holder(frame, upper):
    pair = frame >> 1
    y = pair >> 1
    b = (pair & 1) ^ (y & 1)
    return y, frame & 1, jnp.where(upper == 0, b, 3 - b)


class Sender:
    def __init__(self, ssem, rsem):
        self.ssem, self.rsem, self.used, self.sent = ssem, rsem, 0, []

    def key(self):
        self.used += 1
        return self.used - 1

    def make(self, src, dst, k, to):
        return pltpu.make_async_remote_copy(
            src_ref=src,
            dst_ref=dst,
            send_sem=self.ssem.at[k],
            recv_sem=self.rsem.at[k],
            device_id=to,
            device_id_type=MESH,
        )

    def send(self, src, dst, to, when=None):
        k = self.key()
        copy = self.make(src, dst, k, to)
        if when is None:
            copy.start()
        else:
            pl.when(when)(copy.start)
        self.sent.append((copy, when))
        return k

    def arrived(self, ref, k, when=None):
        copy = pltpu.make_async_copy(ref, ref, self.rsem.at[k])
        if when is None:
            copy.wait()
        else:
            pl.when(when)(copy.wait)

    def drain(self):
        for copy, when in self.sent:
            if when is None:
                copy.wait_send()
            else:
                pl.when(when)(copy.wait_send)
        self.sent = []


def greet(peers):
    barrier = pltpu.get_barrier_semaphore()
    count = 0
    for to, when in peers:
        signal = functools.partial(pl.semaphore_signal, barrier, inc=1, device_id=to, device_id_type=MESH)
        if when is None:
            signal()
            count = count + 1
        else:
            pl.when(when)(signal)
            count = count + when.astype(jnp.int32)
    pl.semaphore_wait(barrier, count)


class WeightGather:
    def __init__(self, sender, own, block, band_a, band_b):
        self.s, self.own = sender, own
        self.block, self.band_a, self.band_b = block, band_a, band_b
        self.y, self.c, self.x, self.z = place()
        self.xp, self.xm = (self.x + 1) % NX, (self.x + NX - 1) % NX
        self.yp, self.ym = (self.y + 1) % NY, (self.y + NY - 1) % NY
        self.x2, self.y2 = (self.x + 2) % NX, (self.y + 2) % NY

    def to_x(self, x):
        return dev(self.y, self.c, x, self.z)

    def to_y(self, y):
        return dev(y, self.c, self.x, self.z)

    def stage1(self):
        s, x, y, own = self.s, self.x, self.y, self.own
        a, b = pl.ds(0, HALF), pl.ds(HALF, HALF)
        self.k_axp = s.send(own.at[a], self.block(x, y, a), self.to_x(self.xp))
        self.k_axm = s.send(own.at[a], self.block(x, y, a), self.to_x(self.xm))
        self.k_byp = s.send(own.at[b], self.block(x, y, b), self.to_y(self.yp))
        self.k_bym = s.send(own.at[b], self.block(x, y, b), self.to_y(self.ym))

    def stage1_forward(self):
        s, q = self.s, HALF // 2
        lo, hi = pl.ds(0, q), pl.ds(q, q)
        s.arrived(self.block(self.xm, self.y, pl.ds(0, HALF)), self.k_axp)
        src = self.block(self.xm, self.y, lo)
        self.k_afp = s.send(src, src, self.to_x(self.xp))
        s.arrived(self.block(self.xp, self.y, pl.ds(0, HALF)), self.k_axm)
        src = self.block(self.xp, self.y, hi)
        self.k_afm = s.send(src, src, self.to_x(self.xm))
        lo, hi = pl.ds(HALF, q), pl.ds(HALF + q, q)
        s.arrived(self.block(self.x, self.ym, pl.ds(HALF, HALF)), self.k_byp)
        src = self.block(self.x, self.ym, lo)
        self.k_bfp = s.send(src, src, self.to_y(self.yp))
        s.arrived(self.block(self.x, self.yp, pl.ds(HALF, HALF)), self.k_bym)
        src = self.block(self.x, self.yp, hi)
        self.k_bfm = s.send(src, src, self.to_y(self.ym))

    def stage2(self):
        s, q = self.s, HALF // 2
        s.arrived(self.block(self.x2, self.y, pl.ds(0, q)), self.k_afp)
        s.arrived(self.block(self.x2, self.y, pl.ds(q, q)), self.k_afm)
        band = self.band_a(self.y, None)
        self.k_ayp = s.send(band, band, self.to_y(self.yp))
        self.k_aym = s.send(band, band, self.to_y(self.ym))
        s.arrived(self.block(self.x, self.y2, pl.ds(HALF, q)), self.k_bfp)
        s.arrived(self.block(self.x, self.y2, pl.ds(HALF + q, q)), self.k_bfm)
        band = self.band_b(self.x, None)
        self.k_bxp = s.send(band, band, self.to_x(self.xp))
        self.k_bxm = s.send(band, band, self.to_x(self.xm))
        self.partner(0, self.y, self.x)

    def partner(self, at, y, x):
        other = dev(self.y, 1 - self.c, self.x, self.z)
        a, b = self.band_a(y, None), self.band_b(x, None)
        ka = self.s.send(a, a, other)
        kb = self.s.send(b, b, other)
        self.from_partner = getattr(self, "from_partner", [])
        self.from_partner.append((ka, kb, y, x))

    def stage2_forward(self):
        s = self.s
        s.arrived(self.band_a(self.ym, None), self.k_ayp)
        src = self.band_a(self.ym, 0)
        self.k_a2p = s.send(src, src, self.to_y(self.yp))
        s.arrived(self.band_a(self.yp, None), self.k_aym)
        src = self.band_a(self.yp, 1)
        self.k_a2m = s.send(src, src, self.to_y(self.ym))
        s.arrived(self.band_b(self.xm, None), self.k_bxp)
        src = self.band_b(self.xm, 0)
        self.k_b2p = s.send(src, src, self.to_x(self.xp))
        s.arrived(self.band_b(self.xp, None), self.k_bxm)
        src = self.band_b(self.xp, 1)
        self.k_b2m = s.send(src, src, self.to_x(self.xm))
        self.partner(1, self.ym, self.xm)
        self.partner(2, self.yp, self.xp)

    def stage3(self):
        s = self.s
        for part, k in ((0, self.k_a2p), (1, self.k_a2m)):
            s.arrived(self.band_a(self.y2, part), k)
        for part, k in ((0, self.k_b2p), (1, self.k_b2m)):
            s.arrived(self.band_b(self.x2, part), k)
        self.partner(3, self.y2, self.x2)

    def finish(self):
        for ka, kb, y, x in self.from_partner:
            self.s.arrived(self.band_a(y, None), ka)
            self.s.arrived(self.band_b(x, None), kb)


def block_kernel(
    tok_in, win_in, bin_in, taps_in, cbias_in, wout_in, bout_in, out,
    tok, win, wout0, wout1, ext, act, part, own_par, par, tp, b1, cb1, bout, sendbuf, recvbuf, done,
    lsem, ssem, rsem,
):
    y, c, x, z = place()
    s = Sender(ssem, rsem)
    xs = [(x + d) % NX for d in range(NX)]
    zp, zm = (z + 1) % NZ, (z + NZ - 1) % NZ
    yp, ym = (y + 1) % NY, (y + NY - 1) % NY
    upper = x >> 1
    frame = frame_of(y, c, x)
    last = NY * 4 - 1
    tc, tx = moved_to(y, c, x)
    fc, fx = moved_from(y, c, x)
    stays = (tc == c) & (tx == x)
    moves = jnp.logical_not(stays)
    has_next, has_prev = frame < last, frame > 0
    ny, nc, nx = holder(jnp.minimum(frame + 1, last), upper)
    py, pc, px = holder(jnp.maximum(frame - 1, 0), upper)
    nxt, nxt_other = dev(ny, nc, nx, z), dev(ny, nc, 3 - nx, z)
    prv, prv_other = dev(py, pc, px, z), dev(py, pc, 3 - px, z)
    other_half = dev(y, c, 3 - x, z)

    locals_ = [
        pltpu.make_async_copy(taps_in, tp, lsem.at[0]),
        pltpu.make_async_copy(bin_in, b1, lsem.at[1]),
        pltpu.make_async_copy(cbias_in, cb1, lsem.at[2]),
    ]
    own_bout = pltpu.make_async_copy(bout_in, bout, lsem.at[3])
    for copy in locals_ + [own_bout]:
        copy.start()

    def win_block(x_, y_, rows):
        return win.at[y_, c, rows, pl.ds(x_ * BLK, BLK)]

    def win_a(y_, part_):
        cols = pl.ds(0, CH) if part_ is None else pl.ds(part_ * (CH // 2), CH // 2)
        return win.at[y_, c, pl.ds(0, HALF), cols]

    def win_b(x_, part_):
        ys = pl.ds(0, NY) if part_ is None else pl.ds(part_ * 2, 2)
        return win.at[ys, c, pl.ds(HALF, HALF), pl.ds(x_ * BLK, BLK)]

    g_in = WeightGather(s, win_in, win_block, win_a, win_b)
    own_in = pltpu.make_async_copy(win_in, win_block(x, y, pl.ds(0, BLK)), lsem.at[4])
    own_in.start()

    def out_gather(buf, lo, w, sem):
        def block(x_, y_, rows):
            return buf.at[x_, rows, pl.ds(c * (NY * w) + y_ * w, w)]

        def band_a(y_, part_):
            xs_ = pl.ds(0, NX) if part_ is None else pl.ds(part_ * 2, 2)
            return buf.at[xs_, pl.ds(0, HALF), pl.ds(c * (NY * w) + y_ * w, w)]

        def band_b(x_, part_):
            n = NY * w
            cols = pl.ds(c * n, n) if part_ is None else pl.ds(c * n + part_ * (n // 2), n // 2)
            return buf.at[x_, pl.ds(HALF, HALF), cols]

        own = wout_in.at[:, pl.ds(lo, w)]
        copy = pltpu.make_async_copy(own, block(x, y, pl.ds(0, BLK)), lsem.at[sem])
        copy.start()
        return WeightGather(s, own, block, band_a, band_b), copy

    g0, own0 = out_gather(wout0, 0, 256, 5)
    g1, own1 = out_gather(wout1, 256, 128, 6)

    for copy in locals_:
        copy.wait()
    own_par[0:27, :] = tp[...]
    own_par[27:28, :] = b1[...].reshape(1, BLK)
    own_par[28:29, :] = cb1[...].reshape(1, BLK)

    greet(
        [(dev(y, c, xs[d], z), None) for d in (1, 2, 3)]
        + [(dev(yp, c, x, z), None), (dev(ym, c, x, z), None)]
        + [(dev(y, c, x, zp), None), (dev(y, c, x, zm), None)]
        + [(dev(y, 1 - c, x, z), None)]
        + [(dev(y, tc, tx, z), moves), (dev(y, fc, fx, z), moves)]
        + [(nxt, has_next), (nxt_other, has_next), (prv, has_prev), (prv_other, has_prev)]
        + [(other_half, None)]
    )

    def tok_at(z_, p):
        return tok.at[pl.ds(((z_ + NZ) % NZ) * OWN + p * PIECE, PIECE)]

    home = []
    for p in range(PIECES):
        src = tok_in.at[pl.ds(p * PIECE, PIECE)]
        k = s.send(src, tok_at(z, p), dev(y, tc, tx, z), when=moves)
        stay = pltpu.make_async_copy(src, tok_at(z, p), rsem.at[k])
        pl.when(stays)(stay.start)
        home.append(stay)
    g_in.stage1()

    @pl.when(upper == 0)
    def _():
        ext[:, 0] = jnp.zeros((3, WW, CH), BF16)

    @pl.when(upper == 1)
    def _():
        ext[:, ROWS + 1] = jnp.zeros((3, WW, CH), BF16)

    @pl.when(jnp.logical_not(has_prev))
    def _():
        @pl.loop(0, ROWS + 2)
        def _(r):
            ext[0, r] = jnp.zeros((WW, CH), BF16)

    @pl.when(jnp.logical_not(has_next))
    def _():
        @pl.loop(0, ROWS + 2)
        def _(r):
            ext[2, r] = jnp.zeros((WW, CH), BF16)

    k_tok = {}

    def token_step(d):
        for p in range(PIECES):
            if d == 1:
                home[p].wait()
            for way, to in ((1, zp), (-1, zm)):
                if d == 4 and (p < PIECES // 2) != (way == 1):
                    continue
                src = tok_at(z - way * (d - 1), p)
                if d > 1:
                    s.arrived(src, k_tok[way, d - 1, p])
                k_tok[way, d, p] = s.send(src, src, dev(y, c, x, to))

    def par_at(x_):
        return par.at[:, pl.ds(x_ * BLK, BLK)]

    token_step(1)
    g_in.stage1_forward()
    own_in.wait()
    g_in.stage2()
    k_par = [s.send(own_par, par_at(x), dev(y, c, xs[d], z)) for d in (1, 2, 3)]
    own_copy = pltpu.make_async_copy(own_par, par_at(x), lsem.at[7])
    own_copy.start()
    token_step(2)
    token_step(3)
    g_in.stage2_forward()
    g0.stage1()
    own0.wait()
    g_in.stage3()
    token_step(4)
    g0.stage1_forward()
    own_copy.wait()
    for d in (1, 2, 3):
        s.arrived(par_at((x + NX - d) % NX), k_par[d - 1])
    g_in.finish()
    g0.stage2()
    for p in range(PIECES):
        way = -1 if p < PIECES // 2 else 1
        s.arrived(tok_at(z - way * 3, p), k_tok[way, 3, p])
        s.arrived(tok_at(z + 4, p), k_tok[-way, 4, p])

    src_row = jnp.where(upper == 0, ROWS, 1)
    dst_row = jnp.where(upper == 0, 0, ROWS + 1)
    got_row = jnp.where(upper == 0, ROWS + 1, 0)
    inner = pl.ds(1, ROWS)
    arrivals = []
    step = 256
    for j in range(HALO_CHUNKS):

        @pl.loop(0, HALO_CH // step)
        def _(i):
            cols = pl.ds(pl.multiple_of(j * HALO_CH + i * step, step), step)
            w = win[:, :, :, cols].reshape(D, step)
            before = jnp.dot(tok[...], w, preferred_element_type=F32) + par[27:28, cols]
            ext[1, inner, :, cols] = before.astype(BF16).reshape(ROWS, WW, step)

        cols = pl.ds(j * HALO_CH, HALO_CH)
        frame_src = ext.at[1, inner, :, cols]
        row_src = ext.at[1, src_row, :, cols]
        k1 = s.send(frame_src, ext.at[0, inner, :, cols], nxt, when=has_next)
        k2 = s.send(frame_src, ext.at[2, inner, :, cols], prv, when=has_prev)
        k3 = s.send(row_src, ext.at[1, dst_row, :, cols], other_half)
        k4 = s.send(row_src, ext.at[0, dst_row, :, cols], nxt_other, when=has_next)
        k5 = s.send(row_src, ext.at[2, dst_row, :, cols], prv_other, when=has_prev)
        arrivals.append([
            (ext.at[0, inner, :, cols], k1, has_prev),
            (ext.at[2, inner, :, cols], k2, has_next),
            (ext.at[1, got_row, :, cols], k3, None),
            (ext.at[0, got_row, :, cols], k4, has_prev),
            (ext.at[2, got_row, :, cols], k5, has_next),
        ])
    g0.stage2_forward()
    g1.stage1()
    own1.wait()

    column = lax.broadcasted_iota(jnp.int32, (WW, 128), 0)

    def conv(j):
        for copy in arrivals[j]:
            s.arrived(*copy)

        @pl.loop(0, HALO_CH // 128)
        def _(i):
            lanes = pl.ds(pl.multiple_of(j * HALO_CH + i * 128, 128), 128)

            @pl.loop(0, ROWS)
            def _(r):
                sums = [None, None, None]
                for dt in range(3):
                    for dh in range(3):
                        v = ext[dt, r + dh, :, lanes].astype(F32)
                        for dw in range(3):
                            k = 9 * dt + 3 * dh + dw
                            t = v * par[k : k + 1, lanes]
                            sums[dw] = t if sums[dw] is None else sums[dw] + t
                left = jnp.where(column == 0, 0.0, pltpu.roll(sums[0], 1, 0))
                right = jnp.where(column == WW - 1, 0.0, pltpu.roll(sums[2], WW - 1, 0))
                v = sums[1] + left + right + par[28:29, lanes]
                half = 0.5 * v
                t = jnp.tanh(v * (0.7978845608028654 + 0.035677408136300125 * (v * v)))
                act[pl.ds(pl.multiple_of(r * WW, WW), WW), lanes] = (half + half * t).astype(BF16)

    conv(0)
    g0.stage3()
    g1.stage1_forward()
    conv(1)
    g1.stage2()
    conv(2)
    g1.stage2_forward()
    g0.finish()

    chains = [(q, way, 4 if (q % 2 == 0) == (way == 1) else 3) for q in range(3) for way in (1, -1)]
    slot, n = {}, 0
    for i, (q, way, length) in enumerate(chains):
        for st in range(length):
            slot[i, st] = n
            n += 1
    k_of = {}

    def multiply(q):
        buf, lo = (wout0, q * UNIT) if q < 2 else (wout1, 0)

        @pl.loop(0, UNIT // 256)
        def _(i):
            at = pl.multiple_of(i * 256, 256)
            w = buf[:, :, pl.ds(lo + at, 256)].reshape(CH, 256)
            part[q, :, pl.ds(at, 256)] = jnp.dot(act[...], w, preferred_element_type=F32)

    def pass_on(q, st):
        for i, (q_, way, length) in enumerate(chains):
            if q_ != q or st >= length:
                continue
            at = (z + way * (length - st) + NZ) % NZ
            rows = pl.ds(pl.multiple_of(at * OWN, OWN), OWN)
            value = part[q, rows, :]
            if st > 0:
                got = recvbuf.at[slot[i, st - 1]]
                s.arrived(got, k_of[i, st - 1])
                value = value + got[...].astype(F32)
            mine = slot[i, st]
            sendbuf[mine] = value.astype(BF16)
            to = dev(y, c, x, zp if way == 1 else zm)
            k_of[i, st] = s.send(sendbuf.at[mine], recvbuf.at[mine], to)

    def collect(q):
        rows = pl.ds(pl.multiple_of(z * OWN, OWN), OWN)
        value = part[q, rows, :]
        for i in (2 * q, 2 * q + 1):
            mine = slot[i, chains[i][2] - 1]
            s.arrived(recvbuf.at[mine], k_of[i, chains[i][2] - 1])
            value = value + recvbuf[mine].astype(F32)
        w, lo = (256, 0) if q < 2 else (128, 256)
        for n_ in range(UNIT // w):
            c_, y_ = (q, n_) if q < 2 else (n_ // NY, n_ % NY)
            to = (y_ * 2 + c_) * BLK + lo
            done[:, to : to + w] = (
                value[:, n_ * w : (n_ + 1) * w] + bout[to : to + w].reshape(1, w)
            ).astype(BF16)

    own_bout.wait()
    multiply(0)
    pass_on(0, 0)
    multiply(1)
    pass_on(1, 0)
    pass_on(0, 1)
    g1.stage3()
    g1.finish()
    multiply(2)
    pass_on(2, 0)
    for st in (1, 2, 3):
        for q in range(3):
            if (q, st) != (0, 1):
                pass_on(q, st)
    for q in range(3):
        collect(q)
    k = s.send(done, out, dev(y, fc, fx, z), when=moves)
    stay = pltpu.make_async_copy(done, out, rsem.at[k])
    pl.when(stays)(stay.start)
    stay.wait()
    s.drain()


def body(tokens, w_in, b_in, conv_taps, conv_bias, w_out, b_out):
    keys = 200
    hbm = pl.BlockSpec(memory_space=pl.ANY)
    return pl.pallas_call(
        block_kernel,
        out_shape=jax.ShapeDtypeStruct((OWN, D), BF16),
        in_specs=[hbm] * 7,
        out_specs=hbm,
        scratch_shapes=[
            pltpu.VMEM((GROUP, D), BF16),
            pltpu.VMEM((NY, 2, BLK, CH), BF16),
            pltpu.VMEM((NX, BLK, 2 * NY * 256), BF16),
            pltpu.VMEM((NX, BLK, 2 * NY * 128), BF16),
            pltpu.VMEM((3, ROWS + 2, WW, CH), BF16),
            pltpu.VMEM((GROUP, CH), BF16),
            pltpu.VMEM((3, GROUP, UNIT), F32),
            pltpu.VMEM((32, BLK), F32),
            pltpu.VMEM((32, CH), F32),
            pltpu.VMEM((27, BLK), F32),
            pltpu.VMEM((BLK,), F32),
            pltpu.VMEM((BLK,), F32),
            pltpu.VMEM((D,), F32),
            pltpu.VMEM((21, OWN, UNIT), BF16),
            pltpu.VMEM((21, OWN, UNIT), BF16),
            pltpu.VMEM((OWN, D), BF16),
            pltpu.SemaphoreType.DMA((8,)),
            pltpu.SemaphoreType.DMA((keys,)),
            pltpu.SemaphoreType.DMA((keys,)),
        ],
        compiler_params=pltpu.CompilerParams(
            collective_id=0, has_side_effects=True, vmem_limit_bytes=60 * 2**20
        ),
        name="mix_ffn",
    )(tokens, w_in, b_in, conv_taps, conv_bias, w_out, b_out)


def solution(mesh):
    placed = (
        P(("row", "col"), None),
        P("row", "col"),
        P("col"),
        P(None, "col"),
        P("col"),
        P("col", "row"),
        P(),
    )
    return jax.shard_map(
        body, mesh=mesh, in_specs=placed, out_specs=P(("row", "col"), None), check_vma=False
    )
```

time: 178 us -> 145 us (0.81)
  Pallas kernels: 169 us -> 143 us
  local copies, waits for them, and re-layouts: 7.61 us -> 1.77 us
    pallas_call x3 -> x1, Pallas kernels: 169 us -> 143 us  [body(): pl.pallas_call(block_kernel, out_shape=jax.ShapeDtypeStruct((OWN, D), BF1...]
    unnamed x11 -> x1, local copies, waits for them, and re-layouts: 6.17 us -> 1.77 us
where the time goes in v2:
time: 145 us
  Pallas kernels  143 us (99%)
  local copies, waits for them, and re-layouts  1.77 us (1%)
    pallas_call x1, Pallas kernels, body(): pl.pallas_call(block_kernel, out_shape=jax.ShapeDtypeStruct((OWN, D), BF1...  143 us

profile of v2, /device:TPU:3, one launch (start us, length us, event | category | flops | bytes accessed | tf_op | source)
XLA Modules:
  0.0 144.9 jit_solution(16111191086102354143)
XLA Ops:
  0.0 143.1 %mix_ffn.1 = bf16[64,3072]{1,0:T(8,128)(2,1)} custom-call(bf16[64,3072]{1,0:T(8,128)(2,1)} %tok_in.1, bf16[384,384]{1,0:T(8,128)(2,1)} %win_in.1, f32[384]{0:T(512)} %bin_in.1, f32[27,384]{1,0:T(8,128)} %taps_in.1, f32[384]{0:T(512)} %cbias_in.1, bf16[384,384]{1,0:T(8,128)(2,1)} %wout_in.1, f32[3072]{0:T(1024)} %bout_in.1), custom_call_target="tpu_custom_call" | custom-call | tf_op jit(solution)/shard_map/mix_ffn/pallas_call | solution.py:514
  143.2 1.8 %copy.9 = bf16[64,3072]{1,0:T(8,128)(2,1)} copy(bf16[64,3072]{1,0:T(8,128)(2,1)} %mix_ffn.1) | data formatting | bytes 786432

commit v3 on v2

--- a/solution.py
+++ b/solution.py
@@ -120,97 +120,115 @@
         self.s, self.own = sender, own
         self.block, self.band_a, self.band_b = block, band_a, band_b
         self.y, self.c, self.x, self.z = place()
-        self.xp, self.xm = (self.x + 1) % NX, (self.x + NX - 1) % NX
-        self.yp, self.ym = (self.y + 1) % NY, (self.y + NY - 1) % NY
-        self.x2, self.y2 = (self.x + 2) % NX, (self.y + 2) % NY
-
-    def to_x(self, x):
-        return dev(self.y, self.c, x, self.z)
-
-    def to_y(self, y):
-        return dev(y, self.c, self.x, self.z)
-
-    def stage1(self):
-        s, x, y, own = self.s, self.x, self.y, self.own
-        a, b = pl.ds(0, HALF), pl.ds(HALF, HALF)
-        self.k_axp = s.send(own.at[a], self.block(x, y, a), self.to_x(self.xp))
-        self.k_axm = s.send(own.at[a], self.block(x, y, a), self.to_x(self.xm))
-        self.k_byp = s.send(own.at[b], self.block(x, y, b), self.to_y(self.yp))
-        self.k_bym = s.send(own.at[b], self.block(x, y, b), self.to_y(self.ym))
-
-    def stage1_forward(self):
-        s, q = self.s, HALF // 2
-        lo, hi = pl.ds(0, q), pl.ds(q, q)
-        s.arrived(self.block(self.xm, self.y, pl.ds(0, HALF)), self.k_axp)
-        src = self.block(self.xm, self.y, lo)
-        self.k_afp = s.send(src, src, self.to_x(self.xp))
-        s.arrived(self.block(self.xp, self.y, pl.ds(0, HALF)), self.k_axm)
-        src = self.block(self.xp, self.y, hi)
-        self.k_afm = s.send(src, src, self.to_x(self.xm))
-        lo, hi = pl.ds(HALF, q), pl.ds(HALF + q, q)
-        s.arrived(self.block(self.x, self.ym, pl.ds(HALF, HALF)), self.k_byp)
-        src = self.block(self.x, self.ym, lo)
-        self.k_bfp = s.send(src, src, self.to_y(self.yp))
-        s.arrived(self.block(self.x, self.yp, pl.ds(HALF, HALF)), self.k_bym)
-        src = self.block(self.x, self.yp, hi)
-        self.k_bfm = s.send(src, src, self.to_y(self.ym))
-
-    def stage2(self):
-        s, q = self.s, HALF // 2
-        s.arrived(self.block(self.x2, self.y, pl.ds(0, q)), self.k_afp)
-        s.arrived(self.block(self.x2, self.y, pl.ds(q, q)), self.k_afm)
-        band = self.band_a(self.y, None)
-        self.k_ayp = s.send(band, band, self.to_y(self.yp))
-        self.k_aym = s.send(band, band, self.to_y(self.ym))
-        s.arrived(self.block(self.x, self.y2, pl.ds(HALF, q)), self.k_bfp)
-        s.arrived(self.block(self.x, self.y2, pl.ds(HALF + q, q)), self.k_bfm)
-        band = self.band_b(self.x, None)
-        self.k_bxp = s.send(band, band, self.to_x(self.xp))
-        self.k_bxm = s.send(band, band, self.to_x(self.xm))
-        self.partner(0, self.y, self.x)
-
-    def partner(self, at, y, x):
+        y, c, x, z = self.y, self.c, self.x, self.z
+        self.xs = {"0": x, "+": (x + 1) % NX, "-": (x + NX - 1) % NX, "2": (x + 2) % NX}
+        self.ys = {"0": y, "+": (y + 1) % NY, "-": (y + NY - 1) % NY, "2": (y + 2) % NY}
+        self.to = {
+            "x+": dev(y, c, self.xs["+"], z),
+            "x-": dev(y, c, self.xs["-"], z),
+            "y+": dev(self.ys["+"], c, x, z),
+            "y-": dev(self.ys["-"], c, x, z),
+        }
+        self.keys, self.from_partner = {}, []
+
+    def at(self, place_, lo, hi):
+        return self.block(self.xs[place_[0]], self.ys[place_[1]], pl.ds(lo, hi - lo))
+
+    def push(self, place_, lo, hi, way):
+        src = self.at(place_, lo, hi)
+        self.keys[place_, lo, hi, way] = self.s.send(src, src, self.to[way])
+
+    def pull(self, here, lo, hi, way, there):
+        self.s.arrived(self.at(here, lo, hi), self.keys[there, lo, hi, way])
+
+    def p0(self):
+        for way in ("y+", "y-", "x+", "x-"):
+            self.keys["00", 0, BLK, way] = self.s.send(self.own, self.at("00", 0, BLK), self.to[way])
+
+    def p1y(self):
+        h, q = HALF, HALF // 2
+        self.pull("0-", 0, BLK, "y+", "00")
+        self.push("0-", 0, h + q, "y+")
+        self.push("0-", h, BLK, "x+")
+        self.push("0-", h, BLK, "x-")
+        self.pull("0+", 0, BLK, "y-", "00")
+        self.push("0+", h + q, BLK, "y-")
+        self.push("0+", h, BLK, "x+")
+        self.push("0+", h, BLK, "x-")
+
+    def p1x(self):
+        h, q = HALF, HALF // 2
+        self.pull("-0", 0, BLK, "x+", "00")
+        self.push("-0", q, BLK, "x+")
+        self.push("-0", 0, h, "y+")
+        self.push("-0", 0, h, "y-")
+        self.pull("+0", 0, BLK, "x-", "00")
+        self.push("+0", 0, q, "x-")
+        self.push("+0", 0, h, "y+")
+        self.push("+0", 0, h, "y-")
+
+    def p2y(self):
+        h, q = HALF, HALF // 2
+        self.pull("02", 0, h + q, "y+", "0-")
+        self.pull("02", h + q, BLK, "y-", "0+")
+        self.push("02", h, BLK, "x-")
+        self.push("02", h, BLK, "x+")
+        self.pull("--", 0, h, "y+", "-0")
+        self.push("--", 0, h, "y+")
+        self.pull("++", 0, h, "y-", "+0")
+        self.push("++", 0, h, "y-")
+
+    def p2x(self):
+        h, q = HALF, HALF // 2
+        self.pull("20", q, BLK, "x+", "-0")
+        self.pull("20", 0, q, "x-", "+0")
+        self.push("20", 0, h, "y-")
+        self.push("20", 0, h, "y+")
+        self.pull("--", h, BLK, "x+", "0-")
+        self.push("--", h, BLK, "x+")
+        self.pull("++", h, BLK, "x-", "0+")
+        self.push("++", h, BLK, "x-")
+        self.partner("0", "0")
+
+    def p3(self):
+        h = HALF
+        self.pull("2+", 0, h, "y-", "20")
+        self.push("2+", 0, h, "y-")
+        self.pull("+2", h, BLK, "x-", "02")
+        self.push("+2", h, BLK, "x-")
+        self.pull("+-", 0, h, "y+", "+0")
+        self.pull("-+", 0, h, "y-", "-0")
+        self.pull("-+", h, BLK, "x+", "0+")
+        self.pull("+-", h, BLK, "x-", "0-")
+        self.pull("2-", 0, h, "y+", "20")
+        self.pull("-2", h, BLK, "x+", "02")
+        self.partner("-", "-")
+        self.partner("+", "+")
+
+    def p4(self):
+        h = HALF
+        self.pull("-2", 0, h, "y+", "--")
+        self.pull("2-", h, BLK, "x+", "--")
+        self.pull("+2", 0, h, "y-", "++")
+        self.pull("2+", h, BLK, "x-", "++")
+        self.pull("22", 0, h, "y-", "2+")
+        self.pull("22", h, BLK, "x-", "+2")
+        self.partner("2", "2")
+
+    def partner(self, x, y):
         other = dev(self.y, 1 - self.c, self.x, self.z)
-        a, b = self.band_a(y, None), self.band_b(x, None)
-        ka = self.s.send(a, a, other)
-        kb = self.s.send(b, b, other)
-        self.from_partner = getattr(self, "from_partner", [])
-        self.from_partner.append((ka, kb, y, x))
-
-    def stage2_forward(self):
-        s = self.s
-        s.arrived(self.band_a(self.ym, None), self.k_ayp)
-        src = self.band_a(self.ym, 0)
-        self.k_a2p = s.send(src, src, self.to_y(self.yp))
-        s.arrived(self.band_a(self.yp, None), self.k_aym)
-        src = self.band_a(self.yp, 1)
-        self.k_a2m = s.send(src, src, self.to_y(self.ym))
-        s.arrived(self.band_b(self.xm, None), self.k_bxp)
-        src = self.band_b(self.xm, 0)
-        self.k_b2p = s.send(src, src, self.to_x(self.xp))
-        s.arrived(self.band_b(self.xp, None), self.k_bxm)
-        src = self.band_b(self.xp, 1)
-        self.k_b2m = s.send(src, src, self.to_x(self.xm))
-        self.partner(1, self.ym, self.xm)
-        self.partner(2, self.yp, self.xp)
-
-    def stage3(self):
-        s = self.s
-        for part, k in ((0, self.k_a2p), (1, self.k_a2m)):
-            s.arrived(self.band_a(self.y2, part), k)
-        for part, k in ((0, self.k_b2p), (1, self.k_b2m)):
-            s.arrived(self.band_b(self.x2, part), k)
-        self.partner(3, self.y2, self.x2)
+        a, b = self.band_a(self.ys[y]), self.band_b(self.xs[x])
+        self.from_partner.append((a, self.s.send(a, a, other)))
+        self.from_partner.append((b, self.s.send(b, b, other)))
 
     def finish(self):
-        for ka, kb, y, x in self.from_partner:
-            self.s.arrived(self.band_a(y, None), ka)
-            self.s.arrived(self.band_b(x, None), kb)
+        for ref, k in self.from_partner:
+            self.s.arrived(ref, k)
 
 
 def block_kernel(
     tok_in, win_in, bin_in, taps_in, cbias_in, wout_in, bout_in, out,
-    tok, win, wout0, wout1, ext, act, part, own_par, par, tp, b1, cb1, bout, sendbuf, recvbuf, done,
+    tok, win, wout, ext, act, part, own_par, par, tp, b1, cb1, bout, sendbuf, recvbuf, summed, moved, done,
     lsem, ssem, rsem,
 ):
     y, c, x, z = place()
@@ -244,38 +262,35 @@
     def win_block(x_, y_, rows):
         return win.at[y_, c, rows, pl.ds(x_ * BLK, BLK)]
 
-    def win_a(y_, part_):
-        cols = pl.ds(0, CH) if part_ is None else pl.ds(part_ * (CH // 2), CH // 2)
-        return win.at[y_, c, pl.ds(0, HALF), cols]
-
-    def win_b(x_, part_):
-        ys = pl.ds(0, NY) if part_ is None else pl.ds(part_ * 2, 2)
-        return win.at[ys, c, pl.ds(HALF, HALF), pl.ds(x_ * BLK, BLK)]
+    def win_a(y_):
+        return win.at[y_, c, pl.ds(0, HALF), :]
+
+    def win_b(x_):
+        return win.at[:, c, pl.ds(HALF, HALF), pl.ds(x_ * BLK, BLK)]
 
     g_in = WeightGather(s, win_in, win_block, win_a, win_b)
     own_in = pltpu.make_async_copy(win_in, win_block(x, y, pl.ds(0, BLK)), lsem.at[4])
     own_in.start()
 
-    def out_gather(buf, lo, w, sem):
+    def out_gather(q):
+        w = BLK // 3
+        n = NY * w
+
         def block(x_, y_, rows):
-            return buf.at[x_, rows, pl.ds(c * (NY * w) + y_ * w, w)]
-
-        def band_a(y_, part_):
-            xs_ = pl.ds(0, NX) if part_ is None else pl.ds(part_ * 2, 2)
-            return buf.at[xs_, pl.ds(0, HALF), pl.ds(c * (NY * w) + y_ * w, w)]
-
-        def band_b(x_, part_):
-            n = NY * w
-            cols = pl.ds(c * n, n) if part_ is None else pl.ds(c * n + part_ * (n // 2), n // 2)
-            return buf.at[x_, pl.ds(HALF, HALF), cols]
-
-        own = wout_in.at[:, pl.ds(lo, w)]
-        copy = pltpu.make_async_copy(own, block(x, y, pl.ds(0, BLK)), lsem.at[sem])
+            return wout.at[q, x_, rows, pl.ds(c * n + y_ * w, w)]
+
+        def band_a(y_):
+            return wout.at[q, :, pl.ds(0, HALF), pl.ds(c * n + y_ * w, w)]
+
+        def band_b(x_):
+            return wout.at[q, x_, pl.ds(HALF, HALF), pl.ds(c * n, n)]
+
+        own = wout_in.at[:, pl.ds(q * w, w)]
+        copy = pltpu.make_async_copy(own, block(x, y, pl.ds(0, BLK)), lsem.at[5 + q])
         copy.start()
         return WeightGather(s, own, block, band_a, band_b), copy
 
-    g0, own0 = out_gather(wout0, 0, 256, 5)
-    g1, own1 = out_gather(wout1, 256, 128, 6)
+    (g0, own0), (g1, own1), (g2, own2) = [out_gather(q) for q in range(3)]
 
     for copy in locals_:
         copy.wait()
@@ -303,7 +318,7 @@
         stay = pltpu.make_async_copy(src, tok_at(z, p), rsem.at[k])
         pl.when(stays)(stay.start)
         home.append(stay)
-    g_in.stage1()
+    g_in.p0()
 
     @pl.when(upper == 0)
     def _():
@@ -343,29 +358,31 @@
         return par.at[:, pl.ds(x_ * BLK, BLK)]
 
     token_step(1)
-    g_in.stage1_forward()
-    own_in.wait()
-    g_in.stage2()
+    g_in.p1y()
     k_par = [s.send(own_par, par_at(x), dev(y, c, xs[d], z)) for d in (1, 2, 3)]
-    own_copy = pltpu.make_async_copy(own_par, par_at(x), lsem.at[7])
+    own_copy = pltpu.make_async_copy(own_par, par_at(x), lsem.at[8])
     own_copy.start()
     token_step(2)
+    g_in.p1x()
+    own_in.wait()
+    g_in.p2y()
     token_step(3)
-    g_in.stage2_forward()
-    g0.stage1()
+    g_in.p2x()
+    token_step(4)
+    g_in.p3()
     own0.wait()
-    g_in.stage3()
-    token_step(4)
-    g0.stage1_forward()
+    g0.p0()
     own_copy.wait()
     for d in (1, 2, 3):
         s.arrived(par_at((x + NX - d) % NX), k_par[d - 1])
-    g_in.finish()
-    g0.stage2()
+    g_in.p4()
     for p in range(PIECES):
         way = -1 if p < PIECES // 2 else 1
         s.arrived(tok_at(z - way * 3, p), k_tok[way, 3, p])
         s.arrived(tok_at(z + 4, p), k_tok[-way, 4, p])
+    g0.p1y()
+    g0.p1x()
+    g_in.finish()
 
     src_row = jnp.where(upper == 0, ROWS, 1)
     dst_row = jnp.where(upper == 0, 0, ROWS + 1)
@@ -397,9 +414,14 @@
             (ext.at[0, got_row, :, cols], k4, has_prev),
             (ext.at[2, got_row, :, cols], k5, has_next),
         ])
-    g0.stage2_forward()
-    g1.stage1()
+        if j == 0:
+            g0.p2y()
+            g0.p2x()
+        if j == 1:
+            g0.p3()
     own1.wait()
+    g1.p0()
+    g0.p4()
 
     column = lax.broadcasted_iota(jnp.int32, (WW, 128), 0)
 
@@ -429,12 +451,14 @@
                 act[pl.ds(pl.multiple_of(r * WW, WW), WW), lanes] = (half + half * t).astype(BF16)
 
     conv(0)
-    g0.stage3()
-    g1.stage1_forward()
+    g1.p1y()
+    g1.p1x()
     conv(1)
-    g1.stage2()
+    g1.p2y()
+    g1.p2x()
+    own2.wait()
+    g2.p0()
     conv(2)
-    g1.stage2_forward()
     g0.finish()
 
     chains = [(q, way, 4 if (q % 2 == 0) == (way == 1) else 3) for q in range(3) for way in (1, -1)]
@@ -446,13 +470,11 @@
     k_of = {}
 
     def multiply(q):
-        buf, lo = (wout0, q * UNIT) if q < 2 else (wout1, 0)
-
         @pl.loop(0, UNIT // 256)
         def _(i):
-            at = pl.multiple_of(i * 256, 256)
-            w = buf[:, :, pl.ds(lo + at, 256)].reshape(CH, 256)
-            part[q, :, pl.ds(at, 256)] = jnp.dot(act[...], w, preferred_element_type=F32)
+            cols = pl.ds(pl.multiple_of(i * 256, 256), 256)
+            w = wout[q, :, :, cols].reshape(CH, 256)
+            part[q, :, cols] = jnp.dot(act[...], w, preferred_element_type=F32)
 
     def pass_on(q, st):
         for i, (q_, way, length) in enumerate(chains):
@@ -470,6 +492,8 @@
             to = dev(y, c, x, zp if way == 1 else zm)
             k_of[i, st] = s.send(sendbuf.at[mine], recvbuf.at[mine], to)
 
+    back = []
+
     def collect(q):
         rows = pl.ds(pl.multiple_of(z * OWN, OWN), OWN)
         value = part[q, rows, :]
@@ -477,39 +501,64 @@
             mine = slot[i, chains[i][2] - 1]
             s.arrived(recvbuf.at[mine], k_of[i, chains[i][2] - 1])
             value = value + recvbuf[mine].astype(F32)
-        w, lo = (256, 0) if q < 2 else (128, 256)
+        w = BLK // 3
         for n_ in range(UNIT // w):
-            c_, y_ = (q, n_) if q < 2 else (n_ // NY, n_ % NY)
-            to = (y_ * 2 + c_) * BLK + lo
-            done[:, to : to + w] = (
-                value[:, n_ * w : (n_ + 1) * w] + bout[to : to + w].reshape(1, w)
+            lo = ((n_ % NY) * 2 + n_ // NY) * BLK + q * w
+            summed[q, :, n_ * w : (n_ + 1) * w] = (
+                value[:, n_ * w : (n_ + 1) * w] + bout[lo : lo + w].reshape(1, w)
             ).astype(BF16)
+        k = s.send(summed.at[q], moved.at[q], dev(y, fc, fx, z), when=moves)
+        stay = pltpu.make_async_copy(summed.at[q], moved.at[q], rsem.at[k])
+        pl.when(stays)(stay.start)
+        back.append(stay)
+
+    def put(q):
+        back[q].wait()
+        w = BLK // 3
+        for n_ in range(UNIT // w):
+            lo = ((n_ % NY) * 2 + n_ // NY) * BLK + q * w
+            done[:, lo : lo + w] = moved[q, :, n_ * w : (n_ + 1) * w]
 
     own_bout.wait()
     multiply(0)
     pass_on(0, 0)
+    g1.p3()
+    g2.p1y()
+    g2.p1x()
+    pass_on(0, 1)
+    g1.p4()
+    g2.p2y()
+    g2.p2x()
+    g1.finish()
     multiply(1)
     pass_on(1, 0)
-    pass_on(0, 1)
-    g1.stage3()
-    g1.finish()
+    pass_on(0, 2)
+    g2.p3()
+    pass_on(1, 1)
+    pass_on(0, 3)
+    g2.p4()
+    g2.finish()
     multiply(2)
     pass_on(2, 0)
-    for st in (1, 2, 3):
-        for q in range(3):
-            if (q, st) != (0, 1):
-                pass_on(q, st)
-    for q in range(3):
-        collect(q)
-    k = s.send(done, out, dev(y, fc, fx, z), when=moves)
-    stay = pltpu.make_async_copy(done, out, rsem.at[k])
-    pl.when(stays)(stay.start)
-    stay.wait()
+    pass_on(1, 2)
+    collect(0)
+    pass_on(2, 1)
+    pass_on(1, 3)
+    pass_on(2, 2)
+    collect(1)
+    put(0)
+    pass_on(2, 3)
+    collect(2)
+    put(1)
+    put(2)
+    stored = pltpu.make_async_copy(done, out, lsem.at[9])
+    stored.start()
+    stored.wait()
     s.drain()
 
 
 def body(tokens, w_in, b_in, conv_taps, conv_bias, w_out, b_out):
-    keys = 200
+    keys = 230
     hbm = pl.BlockSpec(memory_space=pl.ANY)
     return pl.pallas_call(
         block_kernel,
@@ -519,8 +568,7 @@
         scratch_shapes=[
             pltpu.VMEM((GROUP, D), BF16),
             pltpu.VMEM((NY, 2, BLK, CH), BF16),
-            pltpu.VMEM((NX, BLK, 2 * NY * 256), BF16),
-            pltpu.VMEM((NX, BLK, 2 * NY * 128), BF16),
+            pltpu.VMEM((3, NX, BLK, UNIT), BF16),
             pltpu.VMEM((3, ROWS + 2, WW, CH), BF16),
             pltpu.VMEM((GROUP, CH), BF16),
             pltpu.VMEM((3, GROUP, UNIT), F32),
@@ -532,8 +580,10 @@
             pltpu.VMEM((D,), F32),
             pltpu.VMEM((21, OWN, UNIT), BF16),
             pltpu.VMEM((21, OWN, UNIT), BF16),
+            pltpu.VMEM((3, OWN, UNIT), BF16),
+            pltpu.VMEM((3, OWN, UNIT), BF16),
             pltpu.VMEM((OWN, D), BF16),
-            pltpu.SemaphoreType.DMA((8,)),
+            pltpu.SemaphoreType.DMA((10,)),
             pltpu.SemaphoreType.DMA((keys,)),
             pltpu.SemaphoreType.DMA((keys,)),
         ],

time: 145 us -> 142 us (0.979)
  Pallas kernels: 143 us -> 140 us
    pallas_call x1, Pallas kernels: 143 us -> 140 us  [body(): pl.pallas_call(block_kernel, out_shape=jax.ShapeDtypeStruct((OWN, D), BF1...]
where the time goes in v3:
time: 142 us
  Pallas kernels  140 us (99%)
  local copies, waits for them, and re-layouts  1.77 us (1%)
    pallas_call x1, Pallas kernels, body(): pl.pallas_call(block_kernel, out_shape=jax.ShapeDtypeStruct((OWN, D), BF1...  140 us

profile of v3, /device:TPU:3, one launch (start us, length us, event | category | flops | bytes accessed | tf_op | source)
XLA Modules:
  0.0 141.7 jit_solution(6519548749664746229)
XLA Ops:
  0.0 139.9 %mix_ffn.1 = bf16[64,3072]{1,0:T(8,128)(2,1)} custom-call(bf16[64,3072]{1,0:T(8,128)(2,1)} %tok_in.1, bf16[384,384]{1,0:T(8,128)(2,1)} %win_in.1, f32[384]{0:T(512)} %bin_in.1, f32[27,384]{1,0:T(8,128)} %taps_in.1, f32[384]{0:T(512)} %cbias_in.1, bf16[384,384]{1,0:T(8,128)(2,1)} %wout_in.1, f32[3072]{0:T(1024)} %bout_in.1), custom_call_target="tpu_custom_call" | custom-call | tf_op jit(solution)/shard_map/mix_ffn/pallas_call | solution.py:563
  139.9 1.8 %copy.9 = bf16[64,3072]{1,0:T(8,128)(2,1)} copy(bf16[64,3072]{1,0:T(8,128)(2,1)} %mix_ffn.1) | data formatting | bytes 786432

commit v4 on v3

--- a/solution.py
+++ b/solution.py
@@ -11,7 +11,8 @@
 NX, NY, NZ = 4, 4, 8
 D = 3072
 BLK = 384
-HALF = BLK // 2
+UPPER_IN = 192
+UPPER_OUT = 192
 CH = NX * BLK
 GROUP = 512
 OWN = 64
@@ -20,7 +21,7 @@
 HALO_CHUNKS = 3
 PIECES = 4
 PIECE = OWN // PIECES
-UNIT = 1024
+UNIT = 512
 HALO_CH = CH // HALO_CHUNKS
 BF16, F32 = jnp.bfloat16, jnp.float32
 
@@ -116,8 +117,10 @@
 
 
 class WeightGather:
-    def __init__(self, sender, own, block, band_a, band_b):
+    def __init__(self, sender, own, block, band_a, band_b, upper, fine):
+        self.fine = fine
         self.s, self.own = sender, own
+        self.h, self.qa, self.qb = upper, upper // 2, upper + (BLK - upper) // 2
         self.block, self.band_a, self.band_b = block, band_a, band_b
         self.y, self.c, self.x, self.z = place()
         y, c, x, z = self.y, self.c, self.x, self.z
@@ -142,80 +145,122 @@
         self.s.arrived(self.at(here, lo, hi), self.keys[there, lo, hi, way])
 
     def p0(self):
-        for way in ("y+", "y-", "x+", "x-"):
-            self.keys["00", 0, BLK, way] = self.s.send(self.own, self.at("00", 0, BLK), self.to[way])
+        h = self.h
+        for lo, hi, ways in ((0, BLK, ("y+", "y-")), (0, h, ("x+", "x-")), (h, BLK, ("x+", "x-"))):
+            for way in ways:
+                src = self.own.at[pl.ds(lo, hi - lo)]
+                self.keys["00", lo, hi, way] = self.s.send(src, self.at("00", lo, hi), self.to[way])
+        if self.fine:
+            other = dev(self.y, 1 - self.c, self.x, self.z)
+            here = self.at("00", 0, BLK)
+            self.from_partner.append((here, self.s.send(self.own, here, other)))
 
     def p1y(self):
-        h, q = HALF, HALF // 2
+        h, qa, qb = self.h, self.qa, self.qb
         self.pull("0-", 0, BLK, "y+", "00")
-        self.push("0-", 0, h + q, "y+")
+        self.push("0-", 0, qb, "y+")
         self.push("0-", h, BLK, "x+")
         self.push("0-", h, BLK, "x-")
+        self.across("0-", 0, BLK)
         self.pull("0+", 0, BLK, "y-", "00")
-        self.push("0+", h + q, BLK, "y-")
+        self.push("0+", qb, BLK, "y-")
         self.push("0+", h, BLK, "x+")
         self.push("0+", h, BLK, "x-")
+        self.across("0+", 0, BLK)
 
     def p1x(self):
-        h, q = HALF, HALF // 2
-        self.pull("-0", 0, BLK, "x+", "00")
-        self.push("-0", q, BLK, "x+")
+        h, qa, qb = self.h, self.qa, self.qb
+        self.pull("-0", 0, h, "x+", "00")
+        self.push("-0", qa, h, "x+")
         self.push("-0", 0, h, "y+")
         self.push("-0", 0, h, "y-")
-        self.pull("+0", 0, BLK, "x-", "00")
-        self.push("+0", 0, q, "x-")
+        self.across("-0", 0, h)
+        self.pull("+0", 0, h, "x-", "00")
+        self.push("+0", 0, qa, "x-")
         self.push("+0", 0, h, "y+")
         self.push("+0", 0, h, "y-")
+        self.across("+0", 0, h)
 
     def p2y(self):
-        h, q = HALF, HALF // 2
-        self.pull("02", 0, h + q, "y+", "0-")
-        self.pull("02", h + q, BLK, "y-", "0+")
+        h, qa, qb = self.h, self.qa, self.qb
+        self.pull("02", 0, qb, "y+", "0-")
+        self.pull("02", qb, BLK, "y-", "0+")
         self.push("02", h, BLK, "x-")
         self.push("02", h, BLK, "x+")
+        self.across("02", 0, BLK)
         self.pull("--", 0, h, "y+", "-0")
         self.push("--", 0, h, "y+")
+        self.across("--", 0, h)
         self.pull("++", 0, h, "y-", "+0")
         self.push("++", 0, h, "y-")
+        self.across("++", 0, h)
 
     def p2x(self):
-        h, q = HALF, HALF // 2
-        self.pull("20", q, BLK, "x+", "-0")
-        self.pull("20", 0, q, "x-", "+0")
+        h, qa, qb = self.h, self.qa, self.qb
+        self.pull("20", qa, h, "x+", "-0")
+        self.pull("20", 0, qa, "x-", "+0")
         self.push("20", 0, h, "y-")
         self.push("20", 0, h, "y+")
+        self.across("20", 0, h)
+        self.pull("-0", h, BLK, "x+", "00")
+        self.push("-0", h, BLK, "x+")
+        self.across("-0", h, BLK)
+        self.pull("+0", h, BLK, "x-", "00")
+        self.across("+0", h, BLK)
         self.pull("--", h, BLK, "x+", "0-")
         self.push("--", h, BLK, "x+")
+        self.across("--", h, BLK)
         self.pull("++", h, BLK, "x-", "0+")
         self.push("++", h, BLK, "x-")
+        self.across("++", h, BLK)
         self.partner("0", "0")
 
     def p3(self):
-        h = HALF
+        h = self.h
         self.pull("2+", 0, h, "y-", "20")
         self.push("2+", 0, h, "y-")
+        self.across("2+", 0, h)
         self.pull("+2", h, BLK, "x-", "02")
         self.push("+2", h, BLK, "x-")
-        self.pull("+-", 0, h, "y+", "+0")
-        self.pull("-+", 0, h, "y-", "-0")
-        self.pull("-+", h, BLK, "x+", "0+")
-        self.pull("+-", h, BLK, "x-", "0-")
-        self.pull("2-", 0, h, "y+", "20")
-        self.pull("-2", h, BLK, "x+", "02")
+        self.across("+2", h, BLK)
+        for here, lo, hi, way, there in (
+            ("+-", 0, h, "y+", "+0"),
+            ("-+", 0, h, "y-", "-0"),
+            ("-+", h, BLK, "x+", "0+"),
+            ("+-", h, BLK, "x-", "0-"),
+            ("2-", 0, h, "y+", "20"),
+            ("-2", h, BLK, "x+", "02"),
+        ):
+            self.pull(here, lo, hi, way, there)
+            self.across(here, lo, hi)
         self.partner("-", "-")
         self.partner("+", "+")
 
     def p4(self):
-        h = HALF
-        self.pull("-2", 0, h, "y+", "--")
-        self.pull("2-", h, BLK, "x+", "--")
-        self.pull("+2", 0, h, "y-", "++")
-        self.pull("2+", h, BLK, "x-", "++")
-        self.pull("22", 0, h, "y-", "2+")
-        self.pull("22", h, BLK, "x-", "+2")
+        h = self.h
+        for here, lo, hi, way, there in (
+            ("20", h, BLK, "x+", "-0"),
+            ("-2", 0, h, "y+", "--"),
+            ("2-", h, BLK, "x+", "--"),
+            ("+2", 0, h, "y-", "++"),
+            ("2+", h, BLK, "x-", "++"),
+            ("22", 0, h, "y-", "2+"),
+            ("22", h, BLK, "x-", "+2"),
+        ):
+            self.pull(here, lo, hi, way, there)
+            self.across(here, lo, hi)
         self.partner("2", "2")
 
+    def across(self, here, lo, hi):
+        if not self.fine:
+            return
+        other = dev(self.y, 1 - self.c, self.x, self.z)
+        ref = self.at(here, lo, hi)
+        self.from_partner.append((ref, self.s.send(ref, ref, other)))
+
     def partner(self, x, y):
+        if self.fine:
+            return
         other = dev(self.y, 1 - self.c, self.x, self.z)
         a, b = self.band_a(self.ys[y]), self.band_b(self.xs[x])
         self.from_partner.append((a, self.s.send(a, a, other)))
@@ -263,12 +308,12 @@
         return win.at[y_, c, rows, pl.ds(x_ * BLK, BLK)]
 
     def win_a(y_):
-        return win.at[y_, c, pl.ds(0, HALF), :]
+        return win.at[y_, c, pl.ds(0, UPPER_IN), :]
 
     def win_b(x_):
-        return win.at[:, c, pl.ds(HALF, HALF), pl.ds(x_ * BLK, BLK)]
-
-    g_in = WeightGather(s, win_in, win_block, win_a, win_b)
+        return win.at[:, c, pl.ds(UPPER_IN, BLK - UPPER_IN), pl.ds(x_ * BLK, BLK)]
+
+    g_in = WeightGather(s, win_in, win_block, win_a, win_b, UPPER_IN, True)
     own_in = pltpu.make_async_copy(win_in, win_block(x, y, pl.ds(0, BLK)), lsem.at[4])
     own_in.start()
 
@@ -280,15 +325,15 @@
             return wout.at[q, x_, rows, pl.ds(c * n + y_ * w, w)]
 
         def band_a(y_):
-            return wout.at[q, :, pl.ds(0, HALF), pl.ds(c * n + y_ * w, w)]
+            return wout.at[q, :, pl.ds(0, UPPER_OUT), pl.ds(c * n + y_ * w, w)]
 
         def band_b(x_):
-            return wout.at[q, x_, pl.ds(HALF, HALF), pl.ds(c * n, n)]
+            return wout.at[q, x_, pl.ds(UPPER_OUT, BLK - UPPER_OUT), pl.ds(c * n, n)]
 
         own = wout_in.at[:, pl.ds(q * w, w)]
         copy = pltpu.make_async_copy(own, block(x, y, pl.ds(0, BLK)), lsem.at[5 + q])
         copy.start()
-        return WeightGather(s, own, block, band_a, band_b), copy
+        return WeightGather(s, own, block, band_a, band_b, UPPER_OUT, False), copy
 
     (g0, own0), (g1, own1), (g2, own2) = [out_gather(q) for q in range(3)]
 
@@ -371,7 +416,11 @@
     token_step(4)
     g_in.p3()
     own0.wait()
+    own1.wait()
+    own2.wait()
     g0.p0()
+    g1.p0()
+    g2.p0()
     own_copy.wait()
     for d in (1, 2, 3):
         s.arrived(par_at((x + NX - d) % NX), k_par[d - 1])
@@ -417,11 +466,6 @@
         if j == 0:
             g0.p2y()
             g0.p2x()
-        if j == 1:
-            g0.p3()
-    own1.wait()
-    g1.p0()
-    g0.p4()
 
     column = lax.broadcasted_iota(jnp.int32, (WW, 128), 0)
 
@@ -451,38 +495,43 @@
                 act[pl.ds(pl.multiple_of(r * WW, WW), WW), lanes] = (half + half * t).astype(BF16)
 
     conv(0)
+    g0.p3()
     g1.p1y()
     g1.p1x()
     conv(1)
+    g0.p4()
+    g2.p1y()
+    g2.p1x()
     g1.p2y()
     g1.p2x()
-    own2.wait()
-    g2.p0()
     conv(2)
     g0.finish()
 
-    chains = [(q, way, 4 if (q % 2 == 0) == (way == 1) else 3) for q in range(3) for way in (1, -1)]
+    units = D // UNIT
+    chains = [
+        (u, way, 4 if (u % 2 == 0) == (way == 1) else 3) for u in range(units) for way in (1, -1)
+    ]
     slot, n = {}, 0
-    for i, (q, way, length) in enumerate(chains):
+    for i, (u, way, length) in enumerate(chains):
         for st in range(length):
             slot[i, st] = n
             n += 1
     k_of = {}
 
     def multiply(q):
-        @pl.loop(0, UNIT // 256)
+        @pl.loop(0, 1024 // 256)
         def _(i):
             cols = pl.ds(pl.multiple_of(i * 256, 256), 256)
             w = wout[q, :, :, cols].reshape(CH, 256)
-            part[q, :, cols] = jnp.dot(act[...], w, preferred_element_type=F32)
-
-    def pass_on(q, st):
-        for i, (q_, way, length) in enumerate(chains):
-            if q_ != q or st >= length:
+            part[2 * q + i // 2, :, pl.ds(pl.multiple_of(i % 2 * 256, 256), 256)] = jnp.dot(act[...], w, preferred_element_type=F32)
+
+    def pass_on(u, st):
+        for i, (u_, way, length) in enumerate(chains):
+            if u_ != u or st >= length:
                 continue
             at = (z + way * (length - st) + NZ) % NZ
             rows = pl.ds(pl.multiple_of(at * OWN, OWN), OWN)
-            value = part[q, rows, :]
+            value = part[u, rows, :]
             if st > 0:
                 got = recvbuf.at[slot[i, st - 1]]
                 s.arrived(got, k_of[i, st - 1])
@@ -494,63 +543,71 @@
 
     back = []
 
-    def collect(q):
+    w = BLK // 3
+
+    def collect(u):
         rows = pl.ds(pl.multiple_of(z * OWN, OWN), OWN)
-        value = part[q, rows, :]
-        for i in (2 * q, 2 * q + 1):
+        value = part[u, rows, :]
+        for i in (2 * u, 2 * u + 1):
             mine = slot[i, chains[i][2] - 1]
             s.arrived(recvbuf.at[mine], k_of[i, chains[i][2] - 1])
             value = value + recvbuf[mine].astype(F32)
-        w = BLK // 3
-        for n_ in range(UNIT // w):
-            lo = ((n_ % NY) * 2 + n_ // NY) * BLK + q * w
-            summed[q, :, n_ * w : (n_ + 1) * w] = (
+        for n_ in range(NY):
+            lo = (n_ * 2 + u % 2) * BLK + u // 2 * w
+            summed[u, :, n_ * w : (n_ + 1) * w] = (
                 value[:, n_ * w : (n_ + 1) * w] + bout[lo : lo + w].reshape(1, w)
             ).astype(BF16)
-        k = s.send(summed.at[q], moved.at[q], dev(y, fc, fx, z), when=moves)
-        stay = pltpu.make_async_copy(summed.at[q], moved.at[q], rsem.at[k])
+        k = s.send(summed.at[u], moved.at[u], dev(y, fc, fx, z), when=moves)
+        stay = pltpu.make_async_copy(summed.at[u], moved.at[u], rsem.at[k])
         pl.when(stays)(stay.start)
         back.append(stay)
 
-    def put(q):
-        back[q].wait()
-        w = BLK // 3
-        for n_ in range(UNIT // w):
-            lo = ((n_ % NY) * 2 + n_ // NY) * BLK + q * w
-            done[:, lo : lo + w] = moved[q, :, n_ * w : (n_ + 1) * w]
+    def put(u):
+        back[u].wait()
+        for n_ in range(NY):
+            lo = (n_ * 2 + u % 2) * BLK + u // 2 * w
+            done[:, lo : lo + w] = moved[u, :, n_ * w : (n_ + 1) * w]
+
+    def hop(q, st):
+        pass_on(2 * q, st)
+        pass_on(2 * q + 1, st)
 
     own_bout.wait()
     multiply(0)
-    pass_on(0, 0)
+    hop(0, 0)
     g1.p3()
-    g2.p1y()
-    g2.p1x()
-    pass_on(0, 1)
-    g1.p4()
     g2.p2y()
     g2.p2x()
+    g1.p4()
+    hop(0, 1)
     g1.finish()
     multiply(1)
-    pass_on(1, 0)
-    pass_on(0, 2)
+    hop(1, 0)
     g2.p3()
-    pass_on(1, 1)
-    pass_on(0, 3)
+    hop(0, 2)
     g2.p4()
+    hop(1, 1)
     g2.finish()
     multiply(2)
-    pass_on(2, 0)
-    pass_on(1, 2)
+    hop(2, 0)
+    hop(0, 3)
+    hop(2, 1)
+    hop(1, 2)
     collect(0)
-    pass_on(2, 1)
-    pass_on(1, 3)
-    pass_on(2, 2)
     collect(1)
+    hop(2, 2)
+    hop(1, 3)
     put(0)
-    pass_on(2, 3)
+    put(1)
+    hop(2, 3)
     collect(2)
-    put(1)
+    collect(3)
+    collect(4)
+    collect(5)
     put(2)
+    put(3)
+    put(4)
+    put(5)
     stored = pltpu.make_async_copy(done, out, lsem.at[9])
     stored.start()
     stored.wait()
@@ -558,7 +615,7 @@
 
 
 def body(tokens, w_in, b_in, conv_taps, conv_bias, w_out, b_out):
-    keys = 230
+    keys = 300
     hbm = pl.BlockSpec(memory_space=pl.ANY)
     return pl.pallas_call(
         block_kernel,
@@ -568,20 +625,20 @@
         scratch_shapes=[
             pltpu.VMEM((GROUP, D), BF16),
             pltpu.VMEM((NY, 2, BLK, CH), BF16),
-            pltpu.VMEM((3, NX, BLK, UNIT), BF16),
+            pltpu.VMEM((3, NX, BLK, 2 * UNIT), BF16),
             pltpu.VMEM((3, ROWS + 2, WW, CH), BF16),
             pltpu.VMEM((GROUP, CH), BF16),
-            pltpu.VMEM((3, GROUP, UNIT), F32),
+            pltpu.VMEM((6, GROUP, UNIT), F32),
             pltpu.VMEM((32, BLK), F32),
             pltpu.VMEM((32, CH), F32),
             pltpu.VMEM((27, BLK), F32),
             pltpu.VMEM((BLK,), F32),
             pltpu.VMEM((BLK,), F32),
             pltpu.VMEM((D,), F32),
-            pltpu.VMEM((21, OWN, UNIT), BF16),
-            pltpu.VMEM((21, OWN, UNIT), BF16),
-            pltpu.VMEM((3, OWN, UNIT), BF16),
-            pltpu.VMEM((3, OWN, UNIT), BF16),
+            pltpu.VMEM((42, OWN, UNIT), BF16),
+            pltpu.VMEM((42, OWN, UNIT), BF16),
+            pltpu.VMEM((6, OWN, UNIT), BF16),
+            pltpu.VMEM((6, OWN, UNIT), BF16),
             pltpu.VMEM((OWN, D), BF16),
             pltpu.SemaphoreType.DMA((10,)),
             pltpu.SemaphoreType.DMA((keys,)),

time: 142 us -> 136 us (0.958)
  Pallas kernels: 140 us -> 134 us
    pallas_call x1, Pallas kernels: 140 us -> 134 us  [body(): pl.pallas_call(block_kernel, out_shape=jax.ShapeDtypeStruct((OWN, D), BF1...]
where the time goes in v4:
time: 136 us
  Pallas kernels  134 us (99%)
  local copies, waits for them, and re-layouts  1.77 us (1%)
    pallas_call x1, Pallas kernels, body(): pl.pallas_call(block_kernel, out_shape=jax.ShapeDtypeStruct((OWN, D), BF1...  134 us

profile of v4, /device:TPU:3, one launch (start us, length us, event | category | flops | bytes accessed | tf_op | source)
XLA Modules:
  0.0 135.8 jit_solution(9947810032098373888)
XLA Ops:
  0.0 134.0 %mix_ffn.1 = bf16[64,3072]{1,0:T(8,128)(2,1)} custom-call(bf16[64,3072]{1,0:T(8,128)(2,1)} %tok_in.1, bf16[384,384]{1,0:T(8,128)(2,1)} %win_in.1, f32[384]{0:T(512)} %bin_in.1, f32[27,384]{1,0:T(8,128)} %taps_in.1, f32[384]{0:T(512)} %cbias_in.1, bf16[384,384]{1,0:T(8,128)(2,1)} %wout_in.1, f32[3072]{0:T(1024)} %bout_in.1), custom_call_target="tpu_custom_call" | custom-call | tf_op jit(solution)/shard_map/mix_ffn/pallas_call | solution.py:620
  134.1 1.8 %copy.9 = bf16[64,3072]{1,0:T(8,128)(2,1)} copy(bf16[64,3072]{1,0:T(8,128)(2,1)} %mix_ffn.1) | data formatting | bytes 786432

commit v5 on v4

--- a/solution.py
+++ b/solution.py
@@ -269,6 +269,92 @@
     def finish(self):
         for ref, k in self.from_partner:
             self.s.arrived(ref, k)
+
+
+class SkewGather(WeightGather):
+    def __init__(self, *rest):
+        super().__init__(*rest)
+        y, c, x, z = self.y, self.c, self.x, self.z
+        to_next = ((x ^ (x >> 1)) ^ y) & 1
+        even = 1 - (x & 1)
+        step_x, step_y = 2 * even - 1, 2 * to_next - 1
+        self.xs["L"], self.xs["U"] = (x + NX + step_x) % NX, (x + NX - step_x) % NX
+        self.ys["L"], self.ys["U"] = (y + NY + step_y) % NY, (y + NY - step_y) % NY
+        self.to = {
+            "xL": dev(y, c, self.xs["L"], z),
+            "xU": dev(y, c, self.xs["U"], z),
+            "yL": dev(self.ys["L"], c, x, z),
+            "yU": dev(self.ys["U"], c, x, z),
+        }
+
+    def p0(self):
+        for way in ("yL", "yU", "xL", "xU"):
+            self.keys["00", 0, BLK, way] = self.s.send(self.own, self.at("00", 0, BLK), self.to[way])
+
+    def p1y(self):
+        h = self.h
+        self.pull("0L", 0, BLK, "yL", "00")
+        self.push("0L", 0, BLK, "yU")
+        self.pull("0U", 0, BLK, "yU", "00")
+        for block in ("0+", "0-"):
+            self.push(block, h, BLK, "xL")
+            self.push(block, h, BLK, "xU")
+
+    def p1x(self):
+        h = self.h
+        self.pull("L0", 0, BLK, "xL", "00")
+        self.push("L0", 0, BLK, "xU")
+        self.push("L0", 0, h, "yL")
+        self.push("L0", 0, h, "yU")
+        self.pull("U0", 0, BLK, "xU", "00")
+        self.push("U0", 0, h, "yL")
+        self.push("U0", 0, h, "yU")
+
+    def p2y(self):
+        h = self.h
+        self.pull("02", 0, BLK, "yU", "0L")
+        self.push("02", h, BLK, "xL")
+        self.push("02", h, BLK, "xU")
+        self.pull("LL", 0, h, "yL", "L0")
+        self.push("LL", 0, h, "yU")
+        self.pull("UL", 0, h, "yL", "U0")
+        self.push("UL", 0, h, "yU")
+
+    def p2x(self):
+        h = self.h
+        self.pull("20", 0, BLK, "xU", "L0")
+        self.push("20", 0, h, "yL")
+        self.push("20", 0, h, "yU")
+        self.pull("L+", h, BLK, "xL", "0+")
+        self.push("L+", h, BLK, "xU")
+        self.pull("L-", h, BLK, "xL", "0-")
+        self.push("L-", h, BLK, "xU")
+        self.partner("0", "0")
+
+    def p3(self):
+        h = self.h
+        self.pull("2L", 0, h, "yL", "20")
+        self.push("2L", 0, h, "yU")
+        self.pull("L2", h, BLK, "xL", "02")
+        self.push("L2", h, BLK, "xU")
+        self.pull("LU", 0, h, "yU", "L0")
+        self.pull("UU", 0, h, "yU", "U0")
+        self.pull("2U", 0, h, "yU", "20")
+        self.pull("U+", h, BLK, "xU", "0+")
+        self.pull("U-", h, BLK, "xU", "0-")
+        self.pull("U2", h, BLK, "xU", "02")
+        self.partner("L", "L")
+        self.partner("U", "U")
+
+    def p4(self):
+        h = self.h
+        self.pull("L2", 0, h, "yU", "LL")
+        self.pull("2+", h, BLK, "xU", "L+")
+        self.pull("U2", 0, h, "yU", "UL")
+        self.pull("2-", h, BLK, "xU", "L-")
+        self.pull("22", 0, h, "yU", "2L")
+        self.pull("22", h, BLK, "xU", "L2")
+        self.partner("2", "2")
 
 
 def block_kernel(
@@ -333,7 +419,7 @@
         own = wout_in.at[:, pl.ds(q * w, w)]
         copy = pltpu.make_async_copy(own, block(x, y, pl.ds(0, BLK)), lsem.at[5 + q])
         copy.start()
-        return WeightGather(s, own, block, band_a, band_b, UPPER_OUT, False), copy
+        return SkewGather(s, own, block, band_a, band_b, UPPER_OUT, False), copy
 
     (g0, own0), (g1, own1), (g2, own2) = [out_gather(q) for q in range(3)]
 
@@ -477,22 +563,29 @@
         def _(i):
             lanes = pl.ds(pl.multiple_of(j * HALO_CH + i * 128, 128), 128)
 
-            @pl.loop(0, ROWS)
+            @pl.loop(0, ROWS, step=2)
             def _(r):
-                sums = [None, None, None]
+                sums = [[None] * 3 for _ in range(2)]
                 for dt in range(3):
-                    for dh in range(3):
-                        v = ext[dt, r + dh, :, lanes].astype(F32)
-                        for dw in range(3):
-                            k = 9 * dt + 3 * dh + dw
-                            t = v * par[k : k + 1, lanes]
-                            sums[dw] = t if sums[dw] is None else sums[dw] + t
-                left = jnp.where(column == 0, 0.0, pltpu.roll(sums[0], 1, 0))
-                right = jnp.where(column == WW - 1, 0.0, pltpu.roll(sums[2], WW - 1, 0))
-                v = sums[1] + left + right + par[28:29, lanes]
-                half = 0.5 * v
-                t = jnp.tanh(v * (0.7978845608028654 + 0.035677408136300125 * (v * v)))
-                act[pl.ds(pl.multiple_of(r * WW, WW), WW), lanes] = (half + half * t).astype(BF16)
+                    for dr in range(2 + 2):
+                        v = ext[dt, r + dr, :, lanes].astype(F32)
+                        for row in range(2):
+                            dh = dr - row
+                            if not 0 <= dh < 3:
+                                continue
+                            for dw in range(3):
+                                k = 9 * dt + 3 * dh + dw
+                                t = v * par[k : k + 1, lanes]
+                                old = sums[row][dw]
+                                sums[row][dw] = t if old is None else old + t
+                for row in range(2):
+                    left = jnp.where(column == 0, 0.0, pltpu.roll(sums[row][0], 1, 0))
+                    right = jnp.where(column == WW - 1, 0.0, pltpu.roll(sums[row][2], WW - 1, 0))
+                    v = sums[row][1] + left + right + par[28:29, lanes]
+                    half = 0.5 * v
+                    t = jnp.tanh(v * (0.7978845608028654 + 0.035677408136300125 * (v * v)))
+                    to = pl.ds(pl.multiple_of((r + row) * WW, WW), WW)
+                    act[to, lanes] = (half + half * t).astype(BF16)
 
     conv(0)
     g0.p3()
@@ -502,9 +595,9 @@
     g0.p4()
     g2.p1y()
     g2.p1x()
+    conv(2)
     g1.p2y()
     g1.p2x()
-    conv(2)
     g0.finish()
 
     units = D // UNIT

time: 136 us -> 133 us (0.978)
  Pallas kernels: 134 us -> 131 us
    pallas_call x1, Pallas kernels: 134 us -> 131 us  [body(): pl.pallas_call(block_kernel, out_shape=jax.ShapeDtypeStruct((OWN, D), BF1...]
where the time goes in v5:
time: 133 us; the launch traced here: 132 us
  Pallas kernels  131 us (98%)
  local copies, waits for them, and re-layouts  1.77 us (1%)
    pallas_call x1, Pallas kernels, body(): pl.pallas_call(block_kernel, out_shape=jax.ShapeDtypeStruct((OWN, D), BF1...  131 us

profile of v5, /device:TPU:3, one launch (start us, length us, event | category | flops | bytes accessed | tf_op | source)
XLA Modules:
  0.0 132.4 jit_solution(10193048591751214504)
XLA Ops:
  0.0 130.7 %mix_ffn.1 = bf16[64,3072]{1,0:T(8,128)(2,1)} custom-call(bf16[64,3072]{1,0:T(8,128)(2,1)} %tok_in.1, bf16[384,384]{1,0:T(8,128)(2,1)} %win_in.1, f32[384]{0:T(512)} %bin_in.1, f32[27,384]{1,0:T(8,128)} %taps_in.1, f32[384]{0:T(512)} %cbias_in.1, bf16[384,384]{1,0:T(8,128)(2,1)} %wout_in.1, f32[3072]{0:T(1024)} %bout_in.1), custom_call_target="tpu_custom_call" | custom-call | tf_op jit(solution)/shard_map/mix_ffn/pallas_call | solution.py:713
  130.7 1.8 %copy.9 = bf16[64,3072]{1,0:T(8,128)(2,1)} copy(bf16[64,3072]{1,0:T(8,128)(2,1)} %mix_ffn.1) | data formatting | bytes 786432

commit v6 on v5

--- a/solution.py
+++ b/solution.py
@@ -18,11 +18,10 @@
 OWN = 64
 WW = 32
 ROWS = GROUP // WW
-HALO_CHUNKS = 3
+CHUNKS = ((0, 512), (512, 512), (1024, 256), (1280, 256))
 PIECES = 4
 PIECE = OWN // PIECES
 UNIT = 512
-HALO_CH = CH // HALO_CHUNKS
 BF16, F32 = jnp.bfloat16, jnp.float32
 
 
@@ -145,15 +144,18 @@
         self.s.arrived(self.at(here, lo, hi), self.keys[there, lo, hi, way])
 
     def p0(self):
-        h = self.h
-        for lo, hi, ways in ((0, BLK, ("y+", "y-")), (0, h, ("x+", "x-")), (h, BLK, ("x+", "x-"))):
-            for way in ways:
-                src = self.own.at[pl.ds(lo, hi - lo)]
-                self.keys["00", lo, hi, way] = self.s.send(src, self.at("00", lo, hi), self.to[way])
+        self.p0x(((0, BLK, ("y+", "y-")),))
         if self.fine:
             other = dev(self.y, 1 - self.c, self.x, self.z)
             here = self.at("00", 0, BLK)
             self.from_partner.append((here, self.s.send(self.own, here, other)))
+
+    def p0x(self, parts=None):
+        h = self.h
+        for lo, hi, ways in parts or ((0, h, ("x+", "x-")), (h, BLK, ("x+", "x-"))):
+            for way in ways:
+                src = self.own.at[pl.ds(lo, hi - lo)]
+                self.keys["00", lo, hi, way] = self.s.send(src, self.at("00", lo, hi), self.to[way])
 
     def p1y(self):
         h, qa, qb = self.h, self.qa, self.qb
@@ -359,7 +361,7 @@
 
 def block_kernel(
     tok_in, win_in, bin_in, taps_in, cbias_in, wout_in, bout_in, out,
-    tok, win, wout, ext, act, part, own_par, par, tp, b1, cb1, bout, sendbuf, recvbuf, summed, moved, done,
+    tok, win, wout, ext, act, part, own_par, par, tp, b1, cb1, bout, sendbuf, recvbuf, summed, moved, done, relay,
     lsem, ssem, rsem,
 ):
     y, c, x, z = place()
@@ -374,6 +376,9 @@
     fc, fx = moved_from(y, c, x)
     stays = (tc == c) & (tx == x)
     moves = jnp.logical_not(stays)
+    far = ((x == 1) | (x == 2)) & (c == (y & 1))
+    near = jnp.logical_and(moves, jnp.logical_not(far))
+    between = ((x == 0) & (c == 0)) | ((x == NX - 1) & (c == 1))
     has_next, has_prev = frame < last, frame > 0
     ny, nc, nx = holder(jnp.minimum(frame + 1, last), upper)
     py, pc, px = holder(jnp.maximum(frame - 1, 0), upper)
@@ -437,15 +442,20 @@
         + [(dev(y, tc, tx, z), moves), (dev(y, fc, fx, z), moves)]
         + [(nxt, has_next), (nxt_other, has_next), (prv, has_prev), (prv_other, has_prev)]
         + [(other_half, None)]
+        + [(dev(y, tc, jnp.where(x == 1, 0, NX - 1), z), far)]
+        + [(dev(y, y & 1, jnp.where(x == 0, 1, 2), z), between)]
     )
 
     def tok_at(z_, p):
         return tok.at[pl.ds(((z_ + NZ) % NZ) * OWN + p * PIECE, PIECE)]
 
-    home = []
+    home, relays = [], []
     for p in range(PIECES):
         src = tok_in.at[pl.ds(p * PIECE, PIECE)]
-        k = s.send(src, tok_at(z, p), dev(y, tc, tx, z), when=moves)
+        stop = relay.at[pl.ds(p * PIECE, PIECE)]
+        k = s.send(src, tok_at(z, p), dev(y, tc, tx, z), when=near)
+        k_stop = s.send(src, stop, dev(y, tc, jnp.where(x == 1, 0, NX - 1), z), when=far)
+        relays.append((stop, k_stop, k))
         stay = pltpu.make_async_copy(src, tok_at(z, p), rsem.at[k])
         pl.when(stays)(stay.start)
         home.append(stay)
@@ -473,9 +483,25 @@
 
     k_tok = {}
 
-    def token_step(d):
-        for p in range(PIECES):
+    def pass_relay(p):
+        stop, k_stop, k = relays[p]
+        s.arrived(stop, k_stop, between)
+        onward = pltpu.make_async_remote_copy(
+            src_ref=stop,
+            dst_ref=tok_at(z, p),
+            send_sem=s.ssem.at[s.key()],
+            recv_sem=s.rsem.at[k],
+            device_id=other_half,
+            device_id_type=MESH,
+        )
+        pl.when(between)(onward.start)
+        s.sent.append((onward, between))
+
+    def token_step(d, first=0, last=PIECES):
+        for p in range(first, last):
             if d == 1:
+                if p > 0:
+                    pass_relay(p - 1)
                 home[p].wait()
             for way, to in ((1, zp), (-1, zm)):
                 if d == 4 and (p < PIECES // 2) != (way == 1):
@@ -489,28 +515,33 @@
         return par.at[:, pl.ds(x_ * BLK, BLK)]
 
     token_step(1)
+    pass_relay(PIECES - 1)
+    g_in.p0x()
     g_in.p1y()
+    token_step(2, 0, 2)
+    g_in.p1x()
+    token_step(2, 2)
+    own_in.wait()
+    token_step(3, 0, 1)
+    g_in.p2y()
+    token_step(3, 1)
+    g_in.p2x()
+    token_step(4, 0, 2)
+    g_in.p3()
     k_par = [s.send(own_par, par_at(x), dev(y, c, xs[d], z)) for d in (1, 2, 3)]
     own_copy = pltpu.make_async_copy(own_par, par_at(x), lsem.at[8])
     own_copy.start()
-    token_step(2)
-    g_in.p1x()
-    own_in.wait()
-    g_in.p2y()
-    token_step(3)
-    g_in.p2x()
-    token_step(4)
-    g_in.p3()
     own0.wait()
     own1.wait()
     own2.wait()
     g0.p0()
     g1.p0()
     g2.p0()
+    token_step(4, 2)
+    g_in.p4()
     own_copy.wait()
     for d in (1, 2, 3):
         s.arrived(par_at((x + NX - d) % NX), k_par[d - 1])
-    g_in.p4()
     for p in range(PIECES):
         way = -1 if p < PIECES // 2 else 1
         s.arrived(tok_at(z - way * 3, p), k_tok[way, 3, p])
@@ -525,16 +556,16 @@
     inner = pl.ds(1, ROWS)
     arrivals = []
     step = 256
-    for j in range(HALO_CHUNKS):
-
-        @pl.loop(0, HALO_CH // step)
+    for j, (first, many) in enumerate(CHUNKS):
+
+        @pl.loop(0, many // step)
         def _(i):
-            cols = pl.ds(pl.multiple_of(j * HALO_CH + i * step, step), step)
+            cols = pl.ds(pl.multiple_of(first + i * step, step), step)
             w = win[:, :, :, cols].reshape(D, step)
             before = jnp.dot(tok[...], w, preferred_element_type=F32) + par[27:28, cols]
             ext[1, inner, :, cols] = before.astype(BF16).reshape(ROWS, WW, step)
 
-        cols = pl.ds(j * HALO_CH, HALO_CH)
+        cols = pl.ds(first, many)
         frame_src = ext.at[1, inner, :, cols]
         row_src = ext.at[1, src_row, :, cols]
         k1 = s.send(frame_src, ext.at[0, inner, :, cols], nxt, when=has_next)
@@ -556,12 +587,13 @@
     column = lax.broadcasted_iota(jnp.int32, (WW, 128), 0)
 
     def conv(j):
+        first, many = CHUNKS[j]
         for copy in arrivals[j]:
             s.arrived(*copy)
 
-        @pl.loop(0, HALO_CH // 128)
+        @pl.loop(0, many // 128)
         def _(i):
-            lanes = pl.ds(pl.multiple_of(j * HALO_CH + i * 128, 128), 128)
+            lanes = pl.ds(pl.multiple_of(first + i * 128, 128), 128)
 
             @pl.loop(0, ROWS, step=2)
             def _(r):
@@ -596,6 +628,7 @@
     g2.p1y()
     g2.p1x()
     conv(2)
+    conv(3)
     g1.p2y()
     g1.p2x()
     g0.finish()
@@ -611,12 +644,14 @@
             n += 1
     k_of = {}
 
-    def multiply(q):
+    def multiply(q, first=0, many=CH):
         @pl.loop(0, 1024 // 256)
         def _(i):
             cols = pl.ds(pl.multiple_of(i * 256, 256), 256)
-            w = wout[q, :, :, cols].reshape(CH, 256)
-            part[2 * q + i // 2, :, pl.ds(pl.multiple_of(i % 2 * 256, 256), 256)] = jnp.dot(act[...], w, preferred_element_type=F32)
+            w = wout[q, :, :, cols].reshape(CH, 256)[first : first + many]
+            to = (2 * q + i // 2, slice(None), pl.ds(pl.multiple_of(i % 2 * 256, 256), 256))
+            more = jnp.dot(act[:, first : first + many], w, preferred_element_type=F32)
+            part[to] = more if first == 0 else part[to] + more
 
     def pass_on(u, st):
         for i, (u_, way, length) in enumerate(chains):
@@ -733,6 +768,7 @@
             pltpu.VMEM((6, OWN, UNIT), BF16),
             pltpu.VMEM((6, OWN, UNIT), BF16),
             pltpu.VMEM((OWN, D), BF16),
+            pltpu.VMEM((OWN, D), BF16),
             pltpu.SemaphoreType.DMA((10,)),
             pltpu.SemaphoreType.DMA((keys,)),
             pltpu.SemaphoreType.DMA((keys,)),

time: 133 us -> 130 us (0.977)
  Pallas kernels: 131 us -> 128 us
    pallas_call x1, Pallas kernels: 131 us -> 128 us  [body(): pl.pallas_call(block_kernel, out_shape=jax.ShapeDtypeStruct((OWN, D), BF1...]
where the time goes in v6:
time: 130 us
  Pallas kernels  128 us (98%)
  local copies, waits for them, and re-layouts  1.77 us (1%)
    pallas_call x1, Pallas kernels, body(): pl.pallas_call(block_kernel, out_shape=jax.ShapeDtypeStruct((OWN, D), BF1...  128 us

profile of v6, /device:TPU:3, one launch (start us, length us, event | category | flops | bytes accessed | tf_op | source)
XLA Modules:
  0.0 130.0 jit_solution(5395508945532355747)
XLA Ops:
  0.0 128.2 %mix_ffn.1 = bf16[64,3072]{1,0:T(8,128)(2,1)} custom-call(bf16[64,3072]{1,0:T(8,128)(2,1)} %tok_in.1, bf16[384,384]{1,0:T(8,128)(2,1)} %win_in.1, f32[384]{0:T(512)} %bin_in.1, f32[27,384]{1,0:T(8,128)} %taps_in.1, f32[384]{0:T(512)} %cbias_in.1, bf16[384,384]{1,0:T(8,128)(2,1)} %wout_in.1, f32[3072]{0:T(1024)} %bout_in.1), custom_call_target="tpu_custom_call" | custom-call | tf_op jit(solution)/shard_map/mix_ffn/pallas_call | solution.py:748
  128.2 1.8 %copy.9 = bf16[64,3072]{1,0:T(8,128)(2,1)} copy(bf16[64,3072]{1,0:T(8,128)(2,1)} %mix_ffn.1) | data formatting | bytes 786432

commit v7 on v6

--- a/solution.py
+++ b/solution.py
@@ -428,12 +428,6 @@
 
     (g0, own0), (g1, own1), (g2, own2) = [out_gather(q) for q in range(3)]
 
-    for copy in locals_:
-        copy.wait()
-    own_par[0:27, :] = tp[...]
-    own_par[27:28, :] = b1[...].reshape(1, BLK)
-    own_par[28:29, :] = cb1[...].reshape(1, BLK)
-
     greet(
         [(dev(y, c, xs[d], z), None) for d in (1, 2, 3)]
         + [(dev(yp, c, x, z), None), (dev(ym, c, x, z), None)]
@@ -528,6 +522,11 @@
     g_in.p2x()
     token_step(4, 0, 2)
     g_in.p3()
+    for copy in locals_:
+        copy.wait()
+    own_par[0:27, :] = tp[...]
+    own_par[27:28, :] = b1[...].reshape(1, BLK)
+    own_par[28:29, :] = cb1[...].reshape(1, BLK)
     k_par = [s.send(own_par, par_at(x), dev(y, c, xs[d], z)) for d in (1, 2, 3)]
     own_copy = pltpu.make_async_copy(own_par, par_at(x), lsem.at[8])
     own_copy.start()
@@ -628,9 +627,9 @@
     g2.p1y()
     g2.p1x()
     conv(2)
-    conv(3)
     g1.p2y()
     g1.p2x()
+    conv(3)
     g0.finish()
 
     units = D // UNIT
@@ -644,14 +643,12 @@
             n += 1
     k_of = {}
 
-    def multiply(q, first=0, many=CH):
-        @pl.loop(0, 1024 // 256)
+    def multiply(u):
+        @pl.loop(0, UNIT // 256)
         def _(i):
-            cols = pl.ds(pl.multiple_of(i * 256, 256), 256)
-            w = wout[q, :, :, cols].reshape(CH, 256)[first : first + many]
-            to = (2 * q + i // 2, slice(None), pl.ds(pl.multiple_of(i % 2 * 256, 256), 256))
-            more = jnp.dot(act[:, first : first + many], w, preferred_element_type=F32)
-            part[to] = more if first == 0 else part[to] + more
+            at = pl.multiple_of(i * 256, 256)
+            w = wout[u // 2, :, :, pl.ds(u % 2 * UNIT + at, 256)].reshape(CH, 256)
+            part[u, :, pl.ds(at, 256)] = jnp.dot(act[...], w, preferred_element_type=F32)
 
     def pass_on(u, st):
         for i, (u_, way, length) in enumerate(chains):
@@ -702,22 +699,28 @@
 
     own_bout.wait()
     multiply(0)
-    hop(0, 0)
+    pass_on(0, 0)
+    multiply(1)
+    pass_on(1, 0)
     g1.p3()
     g2.p2y()
     g2.p2x()
     g1.p4()
     hop(0, 1)
     g1.finish()
-    multiply(1)
-    hop(1, 0)
+    multiply(2)
+    pass_on(2, 0)
+    multiply(3)
+    pass_on(3, 0)
     g2.p3()
     hop(0, 2)
     g2.p4()
     hop(1, 1)
     g2.finish()
-    multiply(2)
-    hop(2, 0)
+    multiply(4)
+    pass_on(4, 0)
+    multiply(5)
+    pass_on(5, 0)
     hop(0, 3)
     hop(2, 1)
     hop(1, 2)

time: 130 us -> 128 us (0.985)
  Pallas kernels: 128 us -> 126 us
    pallas_call x1, Pallas kernels: 128 us -> 126 us  [body(): pl.pallas_call(block_kernel, out_shape=jax.ShapeDtypeStruct((OWN, D), BF1...]
where the time goes in v7:
time: 128 us
  Pallas kernels  126 us (98%)
  local copies, waits for them, and re-layouts  1.77 us (1%)
    pallas_call x1, Pallas kernels, body(): pl.pallas_call(block_kernel, out_shape=jax.ShapeDtypeStruct((OWN, D), BF1...  126 us

profile of v7, /device:TPU:3, one launch (start us, length us, event | category | flops | bytes accessed | tf_op | source)
XLA Modules:
  0.0 127.6 jit_solution(9194024905335183176)
XLA Ops:
  0.0 125.9 %mix_ffn.1 = bf16[64,3072]{1,0:T(8,128)(2,1)} custom-call(bf16[64,3072]{1,0:T(8,128)(2,1)} %tok_in.1, bf16[384,384]{1,0:T(8,128)(2,1)} %win_in.1, f32[384]{0:T(512)} %bin_in.1, f32[27,384]{1,0:T(8,128)} %taps_in.1, f32[384]{0:T(512)} %cbias_in.1, bf16[384,384]{1,0:T(8,128)(2,1)} %wout_in.1, f32[3072]{0:T(1024)} %bout_in.1), custom_call_target="tpu_custom_call" | custom-call | tf_op jit(solution)/shard_map/mix_ffn/pallas_call | solution.py:751
  125.9 1.8 %copy.9 = bf16[64,3072]{1,0:T(8,128)(2,1)} copy(bf16[64,3072]{1,0:T(8,128)(2,1)} %mix_ffn.1) | data formatting | bytes 786432

commit v8 on v7

--- a/solution.py
+++ b/solution.py
@@ -12,7 +12,7 @@
 D = 3072
 BLK = 384
 UPPER_IN = 192
-UPPER_OUT = 192
+UPPER_OUT = 224
 CH = NX * BLK
 GROUP = 512
 OWN = 64

time: 128 us -> 128 us (level)
  no operation moved by 1% of the time
where the time goes in v8:
time: 128 us; the launch traced here: 127 us
  Pallas kernels  126 us (98%)
  local copies, waits for them, and re-layouts  1.77 us (1%)
    pallas_call x1, Pallas kernels, body(): pl.pallas_call(block_kernel, out_shape=jax.ShapeDtypeStruct((OWN, D), BF1...  126 us

profile of v8, /device:TPU:3, one launch (start us, length us, event | category | flops | bytes accessed | tf_op | source)
XLA Modules:
  0.0 127.4 jit_solution(264758611736393972)
XLA Ops:
  0.0 125.7 %mix_ffn.1 = bf16[64,3072]{1,0:T(8,128)(2,1)} custom-call(bf16[64,3072]{1,0:T(8,128)(2,1)} %tok_in.1, bf16[384,384]{1,0:T(8,128)(2,1)} %win_in.1, f32[384]{0:T(512)} %bin_in.1, f32[27,384]{1,0:T(8,128)} %taps_in.1, f32[384]{0:T(512)} %cbias_in.1, bf16[384,384]{1,0:T(8,128)(2,1)} %wout_in.1, f32[3072]{0:T(1024)} %bout_in.1), custom_call_target="tpu_custom_call" | custom-call | tf_op jit(solution)/shard_map/mix_ffn/pallas_call | solution.py:751
  125.7 1.8 %copy.9 = bf16[64,3072]{1,0:T(8,128)(2,1)} copy(bf16[64,3072]{1,0:T(8,128)(2,1)} %mix_ffn.1) | data formatting | bytes 786432
